TPU v7x, 128 devices: a whole 4x4x4 slice. The times are simulated.
128 devices in a mesh: lat: 8 (over z, x_lo), lon: 16 (over y, x_hi, core).
Axes of the slice: x: 4 (x_hi: 2, x_lo: 2; x = x_hi * 2 + x_lo), y: 4, z: 4, core: 2. Of those that a mesh axis runs over, the one named last changes fastest.
Arguments:
- state: float32 [2, 6144, 12288], P(None, 'lat', 'lon'), may hold values from -6 to 6
- direction: float32 [2, 6144, 12288], P(None, 'lat', 'lon'), may hold values from -6 to 6
- diffusivity: bfloat16 [6144, 12288], P('lat', 'lon'), may hold values from 0.29882812 to 3
- inverses: bfloat16 [768, 8, 8, 24, 256], P(('lat', 'lon')), may hold values from -1.5 to 3
Outputs:
- preconditioned: float32 [2, 6144, 12288], P(None, 'lat', 'lon')
- jacobian_product: float32 [2, 6144, 12288], P(None, 'lat', 'lon')
All inputs are finite; a program needn't handle non-finite values.
Results may differ from a plain program's by a relative error of at most 0.0003.
Values sent between devices are 32-bit elements; how exact they have to be, the bound alone decides.
A program may use at most 128 MiB of HBM per device.

v0:
```python
import jax
import jax.numpy as jnp
from jax import lax
from jax.sharding import PartitionSpec as P

zonal_tau = 0.1
merid_tau = 0.5
zonal_cap = 16.0
quad_coef = 0.25
step_size = 0.01
highest = lax.Precision.HIGHEST


def split_up(x, dim, length):
    before, after = (x.shape[:dim], x.shape[dim + 1 :])
    return jnp.moveaxis(x.reshape(*before, length, -1, *after), dim, 0)


def piece_ends(length, count):
    step = length // count
    if step >= 8:
        step -= step % 8
    return [step * k for k in range(1, count)]


def in_order(parts, dim):
    shape = list(parts.shape[1:])
    shape[dim] *= parts.shape[0]
    return jnp.moveaxis(parts, 0, dim).reshape(shape)


def several_exchanges(x, axis, pieces, split_dim, concat_dim):
    parts = split_up(x, split_dim, lax.axis_size(axis))
    split_at = max(range(1, max(2, parts.ndim - 1)), key=lambda d: parts.shape[d])
    outs = []
    for piece in jnp.split(parts, piece_ends(parts.shape[split_at], pieces), axis=split_at):
        if piece.size:
            outs.append(lax.all_to_all(piece, axis, split_axis=0, concat_axis=0, tiled=True))
    return in_order(jnp.concatenate(outs, axis=split_at), concat_dim)


def extended(x, sides, width):
    edges = {}
    for axis, dim in sides:
        size, length = (lax.axis_size(axis), x.shape[dim])
        up = [(i, (i + 1) % size) for i in range(size)]
        last = lax.slice_in_dim(x, length - width, length, axis=dim)
        first = lax.slice_in_dim(x, 0, width, axis=dim)
        edges[dim] = (
            lax.ppermute(last, axis, up),
            lax.ppermute(first, axis, [(b, a) for a, b in up]),
        )
    done = []
    for _, dim in sides:
        low, high = edges[dim]
        around = [(width, width) if d in done else (0, 0) for d in range(x.ndim)]
        x = jnp.concatenate([jnp.pad(low, around), x, jnp.pad(high, around)], axis=dim)
        done.append(dim)
    return x


def lat_geometry(first_row, count, total):
    rows = (first_row + jnp.arange(count, dtype=jnp.int32)).astype(jnp.float32)
    limit = jnp.float32(total)
    cell_cos = jnp.sin(jnp.pi * (rows + 0.5) / limit)
    high_face = rows + 1.0
    face_low = jnp.where((rows > 0.0) & (rows < limit), jnp.sin(jnp.pi * rows / limit), 0.0)
    face_high = jnp.where(high_face < limit, jnp.sin(jnp.pi * high_face / limit), 0.0)
    zonal_factor = jnp.minimum(1.0 / (cell_cos * cell_cos), zonal_cap)
    return (cell_cos[:, None], face_low[:, None], face_high[:, None], zonal_factor[:, None])


def tendency(padded, kappa_field, cell_cos, face_low, face_high, zonal_factor):
    centre = padded[:, 1:-1, 1:-1]
    east_cell = padded[:, 1:-1, 2:]
    west_cell = padded[:, 1:-1, :-2]
    north_cell = padded[:, 2:, 1:-1]
    south_cell = padded[:, :-2, 1:-1]
    east_flux = (
        zonal_tau
        * zonal_factor
        * (1.0 + quad_coef * jnp.square(0.5 * (centre + east_cell)))
        * (east_cell - centre)
    )
    west_flux = (
        zonal_tau
        * zonal_factor
        * (1.0 + quad_coef * jnp.square(0.5 * (centre + west_cell)))
        * (centre - west_cell)
    )
    north_flux = (
        merid_tau
        * face_high
        * (1.0 + quad_coef * jnp.square(0.5 * (centre + north_cell)))
        * (north_cell - centre)
    )
    south_flux = (
        merid_tau
        * face_low
        * (1.0 + quad_coef * jnp.square(0.5 * (centre + south_cell)))
        * (centre - south_cell)
    )
    spread = east_flux - west_flux + (north_flux - south_flux) / cell_cos
    return centre - kappa_field * spread


def batch_apply(table, values):
    batch = values.shape[0]
    wide = jnp.broadcast_to(table, (batch,) + table.shape)
    return lax.dot_general(wide, values, (((2,), (1,)), ((0,), (0,))), precision=highest)


def solve_rows(pencil, inverses):
    items = pencil.shape[0]
    row_count = pencil.shape[1]
    block_rows = inverses.shape[1]
    outer = inverses.shape[3]
    half_inner = inverses.shape[4]
    inner = 2 * half_inner
    length = outer * inner
    outer_ids = jnp.arange(outer, dtype=jnp.int32)
    inner_ids = jnp.arange(inner, dtype=jnp.int32)
    half_ids = jnp.arange(half_inner, dtype=jnp.int32)
    outer_angle = (
        2.0 * jnp.pi * (outer_ids[:, None] * outer_ids[None, :] % outer).astype(jnp.float32) / outer
    )
    outer_cos = jnp.cos(outer_angle)
    outer_sin = jnp.sin(outer_angle)
    twist = (
        2.0
        * jnp.pi
        * (outer_ids[:, None] * inner_ids[None, :] % length).astype(jnp.float32)
        / length
    )
    twist_cos = jnp.cos(twist)
    twist_sin = jnp.sin(twist)
    inner_angle = (
        2.0 * jnp.pi * (inner_ids[:, None] * half_ids[None, :] % inner).astype(jnp.float32) / inner
    )
    inner_cos = jnp.cos(inner_angle)
    inner_sin = jnp.sin(inner_angle)
    forward_table = jnp.concatenate(
        [jnp.concatenate([inner_cos, -inner_sin], 1), jnp.concatenate([inner_sin, inner_cos], 1)], 0
    )
    inverse_table = jnp.concatenate(
        [
            jnp.concatenate([inner_cos.T, inner_sin.T], 1),
            jnp.concatenate([-inner_sin.T, inner_cos.T], 1),
        ],
        0,
    )
    weights = (
        jnp.where((outer_ids[:, None] == 0) & (half_ids[None, :] == 0), 1.0, 2.0).astype(
            jnp.float32
        )
        / length
    )
    grid = pencil.reshape(items * row_count, outer, inner)
    first_re = batch_apply(outer_cos, grid)
    first_im = -batch_apply(outer_sin, grid)
    turned_re = first_re * twist_cos + first_im * twist_sin
    turned_im = first_im * twist_cos - first_re * twist_sin
    spectrum = jnp.dot(jnp.concatenate([turned_re, turned_im], 2), forward_table, precision=highest)
    shape = (items, row_count // block_rows, block_rows, outer, half_inner)
    spec_re = spectrum[..., :half_inner].reshape(shape)
    spec_im = spectrum[..., half_inner:].reshape(shape)
    blocks = inverses.astype(jnp.float32)[None]
    solved_re = jnp.zeros(shape, jnp.float32)
    solved_im = jnp.zeros(shape, jnp.float32)
    for column in range(block_rows):
        factor = blocks[:, :, :, column]
        solved_re = solved_re + factor * spec_re[:, :, column][:, :, None]
        solved_im = solved_im + factor * spec_im[:, :, column][:, :, None]
    solved_re = (solved_re * weights).reshape(items * row_count, outer, half_inner)
    solved_im = (solved_im * weights).reshape(items * row_count, outer, half_inner)
    back = jnp.dot(jnp.concatenate([solved_re, solved_im], 2), inverse_table, precision=highest)
    back_re = back[..., :inner]
    back_im = back[..., inner:]
    rotated_re = back_re * twist_cos - back_im * twist_sin
    rotated_im = back_re * twist_sin + back_im * twist_cos
    values = batch_apply(outer_cos.T, rotated_re) - batch_apply(outer_sin.T, rotated_im)
    return values.reshape(items, row_count, length)


def spectral(direction, inverses):
    pencil = lax.all_to_all(direction, "lon", split_axis=1, concat_axis=2, tiled=True)
    values = solve_rows(pencil, inverses)
    return several_exchanges(values, "lon", 2, 2, 1)


def on_device(state, direction, diffusivity, inverses):
    levels = state.shape[0]
    local_rows = state.shape[1]
    preconditioned = spectral(direction, inverses)
    joined = extended(jnp.concatenate([state, preconditioned], 0), (("lat", 1), ("lon", 2)), 1)
    state_pad = joined[:levels]
    field_pad = joined[levels:]
    geometry = lat_geometry(
        lax.axis_index("lat") * local_rows, local_rows, lax.axis_size("lat") * local_rows
    )
    kappa_field = diffusivity.astype(jnp.float32)
    base = tendency(state_pad, kappa_field, *geometry)
    moved = tendency(state_pad + step_size * field_pad, kappa_field, *geometry)
    jacobian_product = (moved - base) / step_size
    return (preconditioned, jacobian_product)


def solution(mesh):
    return jax.shard_map(
        on_device,
        mesh=mesh,
        in_specs=(
            P(None, "lat", "lon"),
            P(None, "lat", "lon"),
            P("lat", "lon"),
            P(("lat", "lon"), None, None, None, None),
        ),
        out_specs=(P(None, "lat", "lon"), P(None, "lat", "lon")),
        check_vma=False,
    )
```

profile of v0, /device:TPU:0, one launch (start us, length us, event | category | flops | bytes accessed | tf_op | source)
XLA Modules:
  0.0 307.4 jit_solution(14495827092938899645)
XLA Ops:
  0.6 8.2 %copy.24 = f32[2,768,768]{2,0,1:T(2,128)} copy(f32[2,768,768]{2,1,0:T(8,128)} %param.5) | data formatting | bytes 9437184 | tf_op args[1]
  8.8 7.4 %all-to-all-start = ((f32[2,768,768]{2,0,1:T(2,128)}), f32[2,768,768]{2,0,1:T(2,128)}, u32[]{:S(2)}, u32[]{:S(2)}) async-start(f32[2,768,768]{2,0,1:T(2,128)} %copy.24), calls=%async_computation | async-start | bytes 9437184 | tf_op jit(solution)/shard_map/all_to_all | solution.py:186
  16.2 0.7 fusion.94
  16.9 0.1 fusion.95
  16.9 0.9 fusion.87
  17.8 2.7 fusion.81
  20.5 2.7 fusion.82
  23.2 2.9 fusion.79
  26.0 2.9 fusion.77
  28.9 0.7 select_multiply_fusion
  29.6 3.6 %bitcast_convert_fusion = f32[1,6,8,8,24,256]{5,4,3,2,1,0:T(8,128)S(1)} fusion(bf16[6,8,8,24,256]{4,3,2,1,0:T(8,128)(2,1)} %param.7), kind=kLoop, calls=%fused_computation.43 | loop fusion | flops 2359296 | bytes 14155776 | tf_op jit(solution)/shard_map/broadcast_in_dim | solution.py:167
  33.2 2.9 slice_bitcast_fusion.7
  36.1 37.5 %all-to-all-done = f32[2,768,768]{2,0,1:T(2,128)} async-done(((f32[2,768,768]{2,0,1:T(2,128)}), f32[2,768,768]{2,0,1:T(2,128)}, u32[]{:S(2)}, u32[]{:S(2)}) %all-to-all-start) | async-done | bytes 4718624 | tf_op jit(solution)/shard_map/all_to_all | solution.py:186
  73.6 7.3 %copy.37 = f32[2,16,48,768]{3,1,2,0:T(8,128)} copy(f32[2,16,48,768]{3,0,2,1:T(2,128)} %bitcast.2) | data formatting | bytes 9437184 | tf_op jit(solution)/shard_map/all_to_all | solution.py:186
  80.8 6.1 %reshape.189 = f32[96,24,512]{2,1,0:T(8,128)} reshape(f32[2,48,16,768]{3,2,1,0:T(8,128)} %bitcast.87) | data formatting | bytes 9437184 | tf_op jit(solution)/shard_map/reshape | solution.py:158
  86.9 6.3 %fusion.60 = f32[96,24,512]{2,1,0:T(8,128)S(1)} fusion(f32[96,24,512]{2,1,0:T(8,128)} %reshape.189, f32[24,24]{1,0:T(8,128)} %fusion.94), kind=kOutput, calls=%fused_computation.101 | convolution fusion | flops 339738624 | bytes 9439488 | tf_op jit(solution)/shard_map/dot_general | solution.py:110
  93.3 5.6 %multiply_add_fusion = (f32[96,24,512]{2,1,0:T(8,128)S(1)}, f32[96,24,512]{2,1,0:T(8,128)S(1)}) fusion(f32[96,24,512]{2,1,0:T(8,128)S(1)} %fusion.60, f32[24,512]{1,0:T(8,128)S(1)} %copy-done.10, f32[24,512]{1,0:T(8,128)S(1)} %copy-done.11, f32[96,24,512]{2,1,0:T(8,128)S(1)} %copy-done.1, f32[24,24]{1,0:T(8,128)S(1)} %fusion.95), kind=kOutput, calls=%fused_computation.56 | convolution fusion | flops 347996160 | bytes 18974976 | tf_op jit(solution)/shard_map/dot_general | solution.py:110
  99.0 17.2 %fusion = f32[96,24,512]{2,1,0:T(8,128)S(1)} fusion(f32[96,24,512]{2,1,0:T(8,128)S(1)} %get-tuple-element.5, f32[96,24,512]{2,1,0:T(8,128)S(1)} %get-tuple-element.4, f32[512,256]{1,0:T(8,128)S(1)} %copy-done.14, f32[512,256]{1,0:T(8,128)S(1)} %copy-done.13, f32[512,256]{1,0:T(8,128)S(1)} %copy-done.12), kind=kOutput, calls=%fused_computation.1 | convolution fusion | flops 14499446784 | bytes 15728640 | tf_op jit(solution)/shard_map/dot_general | solution.py:163
  116.2 0.4 fusion.102
  116.6 0.3 slice_bitcast_fusion.15
  116.9 0.3 slice_bitcast_fusion.23
  117.2 0.7 copy-done.2
  117.8 0.4 copy-done.3
  118.2 0.4 copy-done.4
  118.6 0.4 copy-done.5
  118.9 0.4 copy-done.6
  119.3 1.5 add_add_fusion
  120.8 1.7 add_add_fusion.1
  122.6 0.3 bitcast_multiply_fusion.1
  122.9 0.7 copy-done.7
  123.6 0.2 copy-done.8
  123.7 0.2 copy-done.9
  123.9 16.8 %fusion.24 = f32[96,24,1024]{2,1,0:T(8,128)S(1)} fusion(f32[96,24,256]{2,1,0:T(8,128)S(1)} %get-tuple-element.39, f32[96,24,256]{2,1,0:T(8,128)S(1)} %get-tuple-element.38, f32[256,512]{1,0:T(8,128)S(1)} %copy-done.9, f32[256,512]{1,0:T(8,128)S(1)} %copy-done.7, f32[256,512]{1,0:T(8,128)S(1)} %copy-done.8), kind=kOutput, calls=%fused_computation.38 | convolution fusion | flops 14498267136 | bytes 15728640 | tf_op jit(solution)/shard_map/dot_general | solution.py:176
  140.7 4.6 %fusion.28 = f32[96,24,512]{2,1,0:T(8,128)S(1)} fusion(f32[96,24,1024]{2,1,0:T(8,128)S(1)} %fusion.24, f32[24,512]{1,0:T(8,128)S(1)} %copy-done.10, f32[24,512]{1,0:T(8,128)S(1)} %copy-done.11, f32[24,24]{1,0:T(8,128)S(1)} %copy-done.15), kind=kOutput, calls=%fused_computation.47 | convolution fusion | flops 343277568 | bytes 14256384 | tf_op jit(solution)/shard_map/dot_general | solution.py:110
  145.4 5.9 %fusion.44 = f32[96,24,512]{2,1,0:T(8,128)} fusion(f32[96,24,512]{2,1,0:T(8,128)S(1)} %fusion.28, f32[96,24,1024]{2,1,0:T(8,128)S(1)} %fusion.24, f32[24,512]{1,0:T(8,128)S(1)} %copy-done.10, f32[24,512]{1,0:T(8,128)S(1)} %copy-done.11, f32[24,24]{1,0:T(8,128)S(1)} %fusion.95), kind=kOutput, calls=%fused_computation.69 | convolution fusion | flops 344457216 | bytes 18974976 | tf_op jit(solution)/shard_map/dot_general | solution.py:110
  151.3 6.3 %reshape_reshape.3 = f32[2,48,16,768]{3,2,1,0:T(8,128)} reshape(f32[96,24,512]{2,1,0:T(8,128)} %fusion.44) | data formatting | bytes 9437184 | tf_op jit(solution)/shard_map/reshape;reshape | solution.py:16
  157.6 5.1 %copy.36 = f32[2,48,16,768]{3,1,0,2:T(8,128)S(1)} copy(f32[2,48,16,768]{3,2,1,0:T(8,128)} %reshape_reshape.3) | data formatting | bytes 9437184 | tf_op jit(solution)/shard_map/reshape;reshape | solution.py:16
  162.7 2.1 fusion.101
  164.8 34.9 %all_to_all.25 = f32[16,2,24,768]{3,2,1,0:T(8,128)S(1)} all-to-all(f32[16,2,24,768]{3,2,1,0:T(8,128)S(1)} %get-tuple-element.18), channel_id=1, replica_groups=mesh['lat'=8,'lon'=16] {'lon'}, dimensions={0} | all-to-all | bytes 4718592 | tf_op jit(solution)/shard_map/all_to_all | solution.py:38
  199.7 4.4 %all-to-all-start.2 = ((f32[16,2,24,768]{3,2,1,0:T(8,128)}), f32[16,2,24,768]{3,2,1,0:T(8,128)}, u32[]{:S(2)}, u32[]{:S(2)}) async-start(f32[16,2,24,768]{3,2,1,0:T(8,128)} %get-tuple-element.19), calls=%async_computation.2 | async-start | bytes 4718592 | tf_op jit(solution)/shard_map/all_to_all | solution.py:38
  204.2 0.1 select_multiply_fusion.1
  204.2 32.0 %all-to-all-done.2 = f32[16,2,24,768]{3,2,1,0:T(8,128)} async-done(((f32[16,2,24,768]{3,2,1,0:T(8,128)}), f32[16,2,24,768]{3,2,1,0:T(8,128)}, u32[]{:S(2)}, u32[]{:S(2)}) %all-to-all-start.2) | async-done | bytes 2359328 | tf_op jit(solution)/shard_map/all_to_all | solution.py:38
  236.3 2.2 pad_maximum_fusion.13
  238.5 0.0 slice-start.3
  238.5 0.4 copy.33
  238.9 0.0 copy-start
  238.9 3.5 %slice-done.3 = s8[4194304]{0:T(1024)(128)(4,1)S(1)} async-done(((s8[4718592]{0:T(1024)(128)(4,1)}), s8[4194304]{0:T(1024)(128)(4,1)S(1)}, s32[]{:S(2)}) %slice-start.3) | async-done | bytes 4194328
  242.4 0.5 pad_maximum_fusion.14
  242.9 0.5 copy.29
  243.4 0.0 collective-permute-start
  243.5 0.5 copy.31
  243.9 5.4 %collective-permute-start.3 = (f32[4,768,1]{1,0,2:T(4,128)S(1)}, f32[4,768,1]{1,0,2:T(4,128)S(1)}, u32[]{:S(2)}, u32[]{:S(2)}) collective-permute-start(f32[4,768,1]{1,0,2:T(4,128)S(1)} %copy.31), channel_id=1, source_target_pairs={{1,0},{2,1},{3,2},{4,3},{5,4},{6,5},{7,6},{8,7},{9,8},{10,9},{11,1... | collective-permute-start | bytes 36872 | tf_op jit(solution)/shard_map/ppermute | solution.py:51
  249.3 0.9 collective-permute-start.1
  250.2 3.5 %collective-permute-start.2 = (f32[4,1,768]{2,1,0:T(1,128)S(1)}, f32[4,1,768]{2,1,0:T(1,128)S(1)}, u32[]{:S(2)}, u32[]{:S(2)}) collective-permute-start(f32[4,1,768]{2,1,0:T(1,128)S(1)} %get-tuple-element.8), channel_id=1, source_target_pairs={{16,0},{32,16},{48,32},{64,48},{80,64},{96,80},{112,96},{0,112},{1... | collective-permute-start | bytes 36872 | tf_op jit(solution)/shard_map/ppermute | solution.py:51
  253.7 3.0 convert_element_type.84
  256.7 0.0 collective-permute-done
  256.7 0.5 copy.30
  257.2 0.2 pad.7
  257.4 1.7 copy.32
  259.0 1.7 pad.8
  260.7 0.0 slice-start.1
  260.8 14.5 %pad_maximum_fusion = f32[4,770,770]{2,1,0:T(8,128)} fusion(f32[4,770,1]{2,1,0:T(8,128)S(1)} %pad.8, f32[4,1,768]{2,1,0:T(1,128)S(1)} %collective-permute-done.2, f32[2,768,768]{2,1,0:T(8,128)} %bitcast.79, f32[2,768,768]{2,1,0:T(8,128)} %param.4, f32[4,1,768]{2,1,0:T(1,128)S(1)} %collective-permute-done.1, f32[4,770,1]{2,1,0:T(8,128)S(1)} %pad.7), kind=kLoop, calls=%fused_computation | loop fusion | flops 11858000 | bytes 18972800 | tf_op jit(solution)/shard_map/concatenate | solution.py:57
  275.3 4.9 %fusion.4 = f32[2,770,770]{2,1,0:T(8,128)S(1)} fusion(f32[4,770,770]{2,1,0:T(8,128)} %pad_maximum_fusion), kind=kLoop, calls=%fused_computation.6 | loop fusion | flops 2371600 | bytes 14229600 | tf_op jit(solution)/shard_map/add | solution.py:203
  280.2 27.0 %subtract_multiply_fusion = f32[2,768,768]{2,1,0:T(8,128)} fusion(f32[2,768,768]{2,1,0:T(8,128)} %param.4, f32[2,768,768]{2,1,0:T(8,128)S(1)} %bitcast.83, f32[4,1,768]{2,1,0:T(1,128)S(1)} %collective-permute-done.1, f32[4,1,768]{2,1,0:T(1,128)S(1)} %collective-permute-done.2, f32[4,770,1]{2,1,0:T(8,128)S(1)} %pad.7, f32[4,770,1]{2,1,0:T(8,128)S(1)} %pad.8, ...), kind=kLoop, calls=%fused_computation.46 | loop fusion | flops 106168320 | bytes 40169536 | tf_op jit(solution)/shard_map/div | solution.py:204
  (39 shorter events, 0.1 us)
Async XLA Ops:
  8.8 64.8 %all-to-all-start = ((f32[2,768,768]{2,0,1:T(2,128)}), f32[2,768,768]{2,0,1:T(2,128)}, u32[]{:S(2)}, u32[]{:S(2)}) async-start(f32[2,768,768]{2,0,1:T(2,128)} %copy.24), calls=%async_computation | async-start | bytes 9437184 | tf_op jit(solution)/shard_map/all_to_all | solution.py:186
  86.9 6.3 %copy-start.1 = (f32[96,24,512]{2,1,0:T(8,128)S(1)}, f32[96,24,512]{2,1,0:T(8,128)}, u32[]{:S(2)}) copy-start(f32[96,24,512]{2,1,0:T(8,128)} %reshape.189) | copy-start | bytes 14155780
  86.9 6.3 %copy-start.10 = (f32[24,512]{1,0:T(8,128)S(1)}, f32[24,512]{1,0:T(8,128)}, u32[]{:S(2)}) copy-start(f32[24,512]{1,0:T(8,128)} %get-tuple-element.40) | copy-start | bytes 147460
  86.9 6.3 %copy-start.11 = (f32[24,512]{1,0:T(8,128)S(1)}, f32[24,512]{1,0:T(8,128)}, u32[]{:S(2)}) copy-start(f32[24,512]{1,0:T(8,128)} %get-tuple-element.41) | copy-start | bytes 147460
  93.3 5.7 %copy-start.12 = (f32[512,256]{1,0:T(8,128)S(1)}, f32[512,256]{1,0:T(8,128)}, u32[]{:S(2)}) copy-start(f32[512,256]{1,0:T(8,128)} %fusion.81) | copy-start | bytes 1572868
  93.3 5.7 %copy-start.13 = (f32[512,256]{1,0:T(8,128)S(1)}, f32[512,256]{1,0:T(8,128)}, u32[]{:S(2)}) copy-start(f32[512,256]{1,0:T(8,128)} %get-tuple-element.42) | copy-start | bytes 1572868
  93.3 5.7 %copy-start.14 = (f32[512,256]{1,0:T(8,128)S(1)}, f32[512,256]{1,0:T(8,128)}, u32[]{:S(2)}) copy-start(f32[512,256]{1,0:T(8,128)} %get-tuple-element.43) | copy-start | bytes 1572868
  116.6 1.3 copy-start.2
  116.6 1.6 copy-start.3
  116.6 2.0 copy-start.4
  116.6 2.3 copy-start.5
  116.6 2.7 copy-start.6
  120.8 1.7 copy-start.16
  122.5 1.0 copy-start.7
  122.6 1.2 copy-start.8
  122.6 1.3 copy-start.9
  123.9 16.8 %copy-start.15 = (f32[24,24]{1,0:T(8,128)S(1)}, f32[24,24]{1,0:T(8,128)}, u32[]{:S(2)}) copy-start(f32[24,24]{1,0:T(8,128)} %fusion.94) | copy-start | bytes 6916
  199.7 36.6 %all-to-all-start.2 = ((f32[16,2,24,768]{3,2,1,0:T(8,128)}), f32[16,2,24,768]{3,2,1,0:T(8,128)}, u32[]{:S(2)}, u32[]{:S(2)}) async-start(f32[16,2,24,768]{3,2,1,0:T(8,128)} %get-tuple-element.19), calls=%async_computation.2 | async-start | bytes 4718592 | tf_op jit(solution)/shard_map/all_to_all | solution.py:38
  236.3 2.6 slice-start.2
  238.5 3.9 %slice-start.3 = ((s8[4718592]{0:T(1024)(128)(4,1)}), s8[4194304]{0:T(1024)(128)(4,1)S(1)}, s32[]{:S(2)}) async-start(s8[4718592]{0:T(1024)(128)(4,1)} %bitcast.84), calls=%async_computation.6 | async-start | bytes 8388608
  238.9 4.0 %copy-start = (f32[16,2,48,768]{3,2,0,1:T(8,128)}, f32[16,2,48,768]{3,2,0,1:T(8,128)S(1)}, u32[]{:S(2)}) copy-start(f32[16,2,48,768]{3,2,0,1:T(8,128)S(1)} %copy.33) | copy-start | bytes 14155780
  243.4 13.3 %collective-permute-start = (f32[4,768,1]{1,0,2:T(4,128)S(1)}, f32[4,768,1]{1,0,2:T(4,128)S(1)}, u32[]{:S(2)}, u32[]{:S(2)}) collective-permute-start(f32[4,768,1]{1,0,2:T(4,128)S(1)} %copy.29), channel_id=1, source_target_pairs={{0,1},{1,2},{2,3},{3,4},{4,5},{5,6},{6,7},{7,8},{8,9},{9,10},{10,1... | collective-permute-start | bytes 36872 | tf_op jit(solution)/shard_map/ppermute | solution.py:50
  243.9 13.4 %collective-permute-start.3 = (f32[4,768,1]{1,0,2:T(4,128)S(1)}, f32[4,768,1]{1,0,2:T(4,128)S(1)}, u32[]{:S(2)}, u32[]{:S(2)}) collective-permute-start(f32[4,768,1]{1,0,2:T(4,128)S(1)} %copy.31), channel_id=1, source_target_pairs={{1,0},{2,1},{3,2},{4,3},{5,4},{6,5},{7,6},{8,7},{9,8},{10,9},{11,1... | collective-permute-start | bytes 36872 | tf_op jit(solution)/shard_map/ppermute | solution.py:51
  249.3 11.4 %collective-permute-start.1 = (f32[4,1,768]{2,1,0:T(1,128)S(1)}, f32[4,1,768]{2,1,0:T(1,128)S(1)}, u32[]{:S(2)}, u32[]{:S(2)}) collective-permute-start(f32[4,1,768]{2,1,0:T(1,128)S(1)} %get-tuple-element.9), channel_id=1, source_target_pairs={{0,16},{16,32},{32,48},{48,64},{64,80},{80,96},{96,112},{112,0},{1... | collective-permute-start | bytes 36872 | tf_op jit(solution)/shard_map/ppermute | solution.py:50
  250.2 10.6 %collective-permute-start.2 = (f32[4,1,768]{2,1,0:T(1,128)S(1)}, f32[4,1,768]{2,1,0:T(1,128)S(1)}, u32[]{:S(2)}, u32[]{:S(2)}) collective-permute-start(f32[4,1,768]{2,1,0:T(1,128)S(1)} %get-tuple-element.8), channel_id=1, source_target_pairs={{16,0},{32,16},{48,32},{64,48},{80,64},{96,80},{112,96},{0,112},{1... | collective-permute-start | bytes 36872 | tf_op jit(solution)/shard_map/ppermute | solution.py:51
  259.0 21.1 %slice-start = ((s8[4718592]{0:T(1024)(128)(4,1)}), s8[4194304]{0:T(1024)(128)(4,1)S(1)}, s32[]{:S(2)}) async-start(s8[4718592]{0:T(1024)(128)(4,1)} %bitcast.81), calls=%async_computation.3 | async-start | bytes 8388608
  260.7 19.4 %slice-start.1 = ((s8[4718592]{0:T(1024)(128)(4,1)}), s8[524288]{0:T(1024)(128)(4,1)S(1)}, s32[]{:S(2)}) async-start(s8[4718592]{0:T(1024)(128)(4,1)} %bitcast.81), calls=%async_computation.4 | async-start | bytes 1048576
where the time goes:
time: 312 us; the launch traced here: 307 us
  other arithmetic  72.7 us (23%)
  waiting for transfers between devices  69.6 us (22%)
  matrix products  56.5 us (18%)
  local copies, waits for them, and re-layouts  50.8 us (16%)
  blocking collectives  34.9 us (11%)
  starting transfers between devices  21.6 us (7%)
    all_to_all x1, waiting for transfers between devices, spectral(): lax.all_to_all(direction, 'lon', split_axis=1, concat_axis=2, tiled=True)  37.5 us
    all_to_all x1, blocking collectives, several_exchanges(): lax.all_to_all(piece, axis, split_axis=0, concat_axis=0, tiled=True)  34.9 us
    all_to_all x1, waiting for transfers between devices, several_exchanges(): lax.all_to_all(piece, axis, split_axis=0, concat_axis=0, tiled=True)  32 us
    div x1, other arithmetic, on_device(): jacobian_product = (moved - base) / step_size  27 us
    dot_general x4, matrix products, batch_apply(): lax.dot_general(wide, values, (((2,), (1,)), ((0,), (0,))), precision=hig...  22.5 us
    dot_general x1, matrix products, solve_rows(): jnp.dot(jnp.concatenate([turned_re, turned_im], 2), forward_table, precis...  17.2 us
    dot_general x1, matrix products, solve_rows(): jnp.dot(jnp.concatenate([solved_re, solved_im], 2), inverse_table, precis...  16.8 us
    unnamed x43, local copies, waits for them, and re-layouts  14.8 us
  transfers between devices with their start and end apart: 6, of which 2 were waited for; matrix products, arithmetic and copies ran while one was open for 9% of the time, Pallas kernels for 0%

commit v1 on v0

v1 whole, which is shorter than its diff:
```python
import functools
import math
import jax
import jax.numpy as jnp
import ml_dtypes
import numpy as np
from jax import lax
from jax.experimental import pallas as pl
from jax.experimental.pallas import tpu as pltpu
from jax.sharding import PartitionSpec as P

OUTER = 24
INNER = 512
HALF = 256


def real_dft(xs):
    n = len(xs)
    if n == 3:
        a, b, c = xs
        t = b + c
        return [(a + t, None), (a - 0.5 * t, (c - b) * math.sin(math.pi / 3))]
    even, odd = (real_dft(xs[0::2]), real_dft(xs[1::2]))
    half = n // 2
    out = [None] * (half + 1)
    out[0] = (even[0][0] + odd[0][0], None)
    out[half] = (even[0][0] - odd[0][0], None)
    for k in range(1, (half + 1) // 2):
        (er, ei), (pr, pi) = (even[k], odd[k])
        c, s = (math.cos(2 * math.pi * k / n), math.sin(2 * math.pi * k / n))
        tr, ti = (pr * c + pi * s, pi * c - pr * s)
        out[k] = (er + tr, ei + ti)
        out[half - k] = (er - tr, ti - ei)
    if half % 2 == 0:
        out[half // 2] = (even[half // 2][0], -odd[half // 2][0])
    return out


def real_dft_back(zs, n):
    if n == 3:
        (c, _), (e, o) = zs
        t, u = (c - 0.5 * e, o * math.sin(math.pi / 3))
        return [c + e, t - u, t + u]
    half = n // 2
    quarter = half // 2
    even = [(zs[0][0] + zs[half][0], None)]
    odd = [(zs[0][0] - zs[half][0], None)]
    for k in range(1, (half + 1) // 2):
        (er, ei), (pr, pi) = (zs[k], zs[half - k])
        even.append((er + pr, ei - pi))
        dr, di = (er - pr, ei + pi)
        c, s = (math.cos(2 * math.pi * k / n), math.sin(2 * math.pi * k / n))
        odd.append((dr * c - di * s, dr * s + di * c))
    if half % 2 == 0:
        even.append((zs[quarter][0], None))
        odd.append((-zs[quarter][1], None))
    first, second = (real_dft_back(even, half), real_dft_back(odd, half))
    return [v for pair in zip(first, second) for v in pair]


def make_tables():
    length = OUTER * INNER
    b = np.arange(INNER)
    q = np.arange(HALF)
    angle = 2 * np.pi * ((b[:, None] * q[None, :]) % INNER) / INNER
    c, s = (np.cos(angle), np.sin(angle))
    table = np.block([[c, -s], [s, c]])
    high = table.astype(ml_dtypes.bfloat16)
    low = (table - high.astype(np.float64)).astype(ml_dtypes.bfloat16)
    twist = 2 * np.pi * ((np.arange(OUTER)[:, None] * b[None, :]) % length) / length
    scale = 2.0 / length
    turns = np.stack(
        [np.cos(twist), np.sin(twist), scale * np.cos(twist), scale * np.sin(twist)]
    ).astype(np.float32)
    weights = np.ones((OUTER, HALF), np.float32)
    weights[0, 0] = 0.5
    return high, low, turns, weights


def split(x):
    high = x.astype(jnp.bfloat16)
    return high, (x - high.astype(jnp.float32)).astype(jnp.bfloat16)


def spectral_chunk(inb, outb, invb, table_hi, table_lo, turns, weights, wide, high, low, narrow, invf):
    levels = 2
    rows = 8

    def widen(k, _):
        invf[k] = invb[k // rows, k % rows].astype(jnp.float32) * weights[...]
        return 0

    lax.fori_loop(0, rows * rows, widen, 0)

    def stage_in(t, _):
        level, tile = (t // 4, t % 4)
        lane = pl.multiple_of(tile * 128, 128)
        xs = [inb[level, :, pl.ds(a * INNER + lane, 128)] for a in range(OUTER)]
        ys = real_dft(xs)
        for p in range(OUTER):
            m = p if p <= OUTER // 2 else OUTER - p
            re, im = ys[m]
            c = turns[0, pl.ds(p, 1), pl.ds(lane, 128)]
            s = turns[1, pl.ds(p, 1), pl.ds(lane, 128)]
            if im is None:
                tr, ti = (re * c, -(re * s))
            elif p <= OUTER // 2:
                tr, ti = (re * c + im * s, im * c - re * s)
            else:
                tr, ti = (re * c - im * s, -(im * c) - re * s)
            where = pl.ds(level * (rows * OUTER) + p, rows, stride=OUTER)
            wide[tile, where, :] = tr
            wide[tile + 4, where, :] = ti
        return 0

    lax.fori_loop(0, 8, stage_in, 0)

    def split_wide(k, _):
        at = pl.ds(pl.multiple_of(k * 32, 32), 32)
        for j in range(8):
            cols = slice(j * 128, j * 128 + 128)
            high[at, cols], low[at, cols] = split(wide[j, at, :])
        return 0

    lax.fori_loop(0, 12, split_wide, 0)

    def forward(n, _):
        cols = pl.ds(pl.multiple_of(n * 256, 256), 256)
        a = jnp.dot(high[...], table_hi[:, cols], preferred_element_type=jnp.float32)
        a += jnp.dot(low[...], table_hi[:, cols], preferred_element_type=jnp.float32)
        a += jnp.dot(high[...], table_lo[:, cols], preferred_element_type=jnp.float32)
        narrow[:, cols] = a
        return 0

    lax.fori_loop(0, 2, forward, 0)

    def solve(t, _):
        pt, lane = (pl.multiple_of((t // 2) * 8, 8), pl.multiple_of((t % 2) * 128, 128))
        spec = [
            [
                narrow[pl.ds((level * rows + s) * OUTER + pt, 8), pl.ds(part * HALF + lane, 128)]
                for level in range(levels)
                for part in range(2)
            ]
            for s in range(rows)
        ]
        for r in range(rows):
            total = [None] * 4
            for s in range(rows):
                factor = invf[r * rows + s, pl.ds(pt, 8), pl.ds(lane, 128)]
                for i in range(4):
                    term = factor * spec[s][i]
                    total[i] = term if total[i] is None else total[i] + term
            for i in range(4):
                level, part = (i // 2, i % 2)
                wide[part * 2 + t % 2, pl.ds((level * rows + r) * OUTER + pt, 8), :] = total[i]
        return 0

    lax.fori_loop(0, 6, solve, 0)

    def split_solved(k, _):
        at = pl.ds(pl.multiple_of(k * 32, 32), 32)
        for j in range(4):
            cols = slice(j * 128, j * 128 + 128)
            high[at, cols], low[at, cols] = split(wide[j, at, :])
        return 0

    lax.fori_loop(0, 12, split_solved, 0)

    def backward(n, _):
        cols = pl.ds(pl.multiple_of(n * 256, 256), 256)
        dims = (((1,), (1,)), ((), ()))
        hi, lo = (high[:, : 2 * HALF], low[:, : 2 * HALF])
        a = lax.dot_general(hi, table_hi[cols, :], dims, preferred_element_type=jnp.float32)
        a += lax.dot_general(lo, table_hi[cols, :], dims, preferred_element_type=jnp.float32)
        a += lax.dot_general(hi, table_lo[cols, :], dims, preferred_element_type=jnp.float32)
        wide[2 * n] = a[:, :128]
        wide[2 * n + 1] = a[:, 128:]
        return 0

    lax.fori_loop(0, 4, backward, 0)

    def stage_out(t, _):
        level, tile = (t // 4, t % 4)
        lane = pl.multiple_of(tile * 128, 128)

        def turned(p):
            where = pl.ds(level * (rows * OUTER) + p, rows, stride=OUTER)
            re = wide[tile, where, :]
            im = wide[tile + 4, where, :]
            c = turns[2, pl.ds(p, 1), pl.ds(lane, 128)]
            s = turns[3, pl.ds(p, 1), pl.ds(lane, 128)]
            return re * c - im * s, re * s + im * c

        zs = []
        for p in range(OUTER // 2 + 1):
            re, im = turned(p)
            if 0 < p < OUTER // 2:
                other_re, other_im = turned(OUTER - p)
                re, im = (re + other_re, im - other_im)
            zs.append((re, im))
        for a, v in enumerate(real_dft_back(zs, OUTER)):
            outb[level, :, pl.ds(a * INNER + lane, 128)] = v
        return 0

    lax.fori_loop(0, 8, stage_out, 0)


zonal_tau = 0.1
merid_tau = 0.5
zonal_cap = 16.0
quad_coef = 0.25
step_size = 0.01
MESH = pl.DeviceIdType.MESH


def make_geometry(bands, members, rows_each):
    total = bands * members * rows_each
    row = np.arange(total, dtype=np.float64)
    cell = np.sin(np.pi * (row + 0.5) / total)
    low = np.where(row > 0, np.sin(np.pi * row / total), 0.0)
    high = np.where(row + 1 < total, np.sin(np.pi * (row + 1) / total), 0.0)
    zonal = zonal_tau * np.minimum(1.0 / (cell * cell), zonal_cap)
    kinds = np.stack([zonal, merid_tau * high / cell, merid_tau * low / cell], -1)
    kinds = kinds.reshape(bands, members, rows_each, 3).transpose(0, 2, 1, 3)
    table = np.zeros((bands, rows_each, members, 8), np.float32)
    table[..., :3] = kinds
    return table.reshape(bands, rows_each, members * 8)


def exchange_kernel(
    bands, members, chunks,
    state, direction, inverses, table_hi_in, table_lo_in, turns_in, weights_in,
    pre, srow, prow, scol, pcol,
    inb, outb, invb, table_hi, table_lo, turns, weights,
    wide, high, low, narrow, invf, edges, scol_out, pcol_out,
    load_sem, edge_sem, own_in, own_out, own_col, send_in, recv_in, send_out, recv_out,
    send_row, recv_row, send_col, recv_col, send_halo, recv_halo,
):
    levels = state.shape[0]
    local_rows = state.shape[1]
    width = state.shape[2]
    rows = 8
    share = chunks * rows
    la, me = (lax.axis_index("lat"), lax.axis_index("lon"))
    up, down = (lax.rem(la + 1, bands), lax.rem(la + bands - 1, bands))
    east, west = (lax.rem(me + 1, members), lax.rem(me + members - 1, members))

    def peer(k):
        y = lax.rem(me // 4 + k // 4, members // 4)
        x = lax.rem(me // 2 + k // 2, 2)
        core = lax.rem(me + k, 2)
        return y * 4 + x * 2 + core

    def remote(src, dst, send, recv, lat, lon):
        return pltpu.make_async_remote_copy(
            src_ref=src, dst_ref=dst, send_sem=send, recv_sem=recv,
            device_id=(lat, lon), device_id_type=MESH,
        )

    barrier = pltpu.get_barrier_semaphore()
    for k in range(1, members):
        pl.semaphore_signal(barrier, inc=1, device_id=(la, peer(k)), device_id_type=MESH)
    for lat in (up, down):
        pl.semaphore_signal(barrier, inc=1, device_id=(lat, me), device_id_type=MESH)

    edge_copies = [
        pltpu.make_async_copy(state.at[:, :, pl.ds(at, 128)], edges.at[side], edge_sem.at[side])
        for side, at in enumerate((0, width - 128))
    ]
    loads = [
        pltpu.make_async_copy(src, dst, load_sem.at[i])
        for i, (src, dst) in enumerate(
            (
                (table_hi_in, table_hi), (table_lo_in, table_lo), (turns_in, turns),
                (weights_in, weights), (inverses, invb),
            )
        )
    ]
    for copy in edge_copies + loads:
        copy.start()
    pl.semaphore_wait(barrier, members + 1)

    def chunk_of(i):
        return lax.rem(i + chunks - 1, chunks)

    def lines(member, c):
        return pl.ds(pl.multiple_of(member * share + c * rows, rows), rows)

    def columns(member):
        return pl.ds(pl.multiple_of(member * width, width), width)

    def send_inputs(i, _):
        c = chunk_of(i)
        for k in range(1, members):
            p = peer(k)
            remote(
                direction.at[:, lines(p, c), :], inb.at[c, :, :, columns(me)],
                send_in, recv_in.at[c], la, p,
            ).start()
        pltpu.make_async_copy(
            direction.at[:, lines(me, c), :], inb.at[c, :, :, columns(me)], own_in.at[c]
        ).start()
        return 0

    lax.fori_loop(0, chunks, send_inputs, 0)
    state_rows = [
        remote(state.at[:, pl.ds(local_rows - rows, rows), :], srow.at[0], send_row.at[0], recv_row.at[0], up, me),
        remote(state.at[:, pl.ds(0, rows), :], srow.at[1], send_row.at[1], recv_row.at[1], down, me),
    ]
    for copy in state_rows:
        copy.start()

    lane = lax.broadcasted_iota(jnp.int32, (rows, 128), 1)
    for copy in edge_copies:
        copy.wait()
    scol_out[...] = jnp.zeros_like(scol_out)

    def pack_state(t, _):
        at = (t // chunks) * 8 + lax.rem(t, chunks)
        for side, first in enumerate((0, 127)):
            for level in range(levels):
                value = edges[side, level, pl.ds(pl.multiple_of(t * rows, rows), rows), :]
                value = pltpu.roll(value, lax.rem(at + 128 - first, 128), 1)
                line = pl.ds(level * rows, rows)
                scol_out[side, line, :] = jnp.where(lane == at, value, scol_out[side, line, :])
        return 0

    lax.fori_loop(0, members * chunks, pack_state, 0)
    pcol_out[...] = jnp.zeros_like(pcol_out)
    state_cols = [
        remote(scol_out.at[1], scol.at[0], send_col.at[0], recv_col.at[0], la, east),
        remote(scol_out.at[0], scol.at[1], send_col.at[1], recv_col.at[1], la, west),
    ]
    for copy in state_cols:
        copy.start()
    for copy in loads:
        copy.wait()

    def arrived(c, sem):
        part = inb.at[c, :, :, pl.ds(0, (members - 1) * width)]
        pltpu.make_async_copy(part, part, sem.at[c]).wait()

    def chunk(i, _):
        c = chunk_of(i)
        arrived(c, recv_in)
        pltpu.make_async_copy(
            direction.at[:, lines(me, c), :], inb.at[c, :, :, columns(me)], own_in.at[c]
        ).wait()
        spectral_chunk(
            inb.at[c], outb.at[c], invb.at[c], table_hi, table_lo, turns, weights,
            wide, high, low, narrow, invf,
        )
        for k in range(1, members):
            p = peer(k)
            remote(
                outb.at[c, :, :, columns(p)], pre.at[:, lines(me, c), :],
                send_out, recv_out.at[c], la, p,
            ).start()
        pltpu.make_async_copy(
            outb.at[c, :, :, columns(me)], pre.at[:, lines(me, c), :], own_out.at[c]
        ).start()

        def pack(d, _):
            tile = width // 128
            before = lax.rem(d * tile + members * tile - 1, members * tile)
            after = lax.rem(d * tile + tile, members * tile)
            held = pcol_out[d]
            for level in range(levels):
                for side, (source, first) in enumerate(((before, 127), (after, 0))):
                    at = c * 4 + level * 2 + side
                    value = outb[c, level, :, pl.ds(pl.multiple_of(source * 128, 128), 128)]
                    value = pltpu.roll(value, lax.rem(at + 128 - first, 128), 1)
                    held = jnp.where(lane == at, value, held)
            pcol_out[d] = held
            return 0

        lax.fori_loop(0, members, pack, 0)
        return 0

    lax.fori_loop(0, chunks, chunk, 0)

    for k in range(1, members):
        p = peer(k)
        remote(pcol_out.at[p], pcol.at[me], send_halo, recv_halo, la, p).start()
    own_halo = pltpu.make_async_copy(pcol_out.at[me], pcol.at[me], own_col)
    own_halo.start()

    def landed(c):
        arrived(c, recv_out)
        pltpu.make_async_copy(
            outb.at[c, :, :, columns(me)], pre.at[:, lines(me, c), :], own_out.at[c]
        ).wait()

    landed(chunks - 1)
    first = remote(pre.at[:, pl.ds(local_rows - rows, rows), :], prow.at[0], send_row.at[2], recv_row.at[2], up, me)
    first.start()
    landed(0)
    second = remote(pre.at[:, pl.ds(0, rows), :], prow.at[1], send_row.at[3], recv_row.at[3], down, me)
    second.start()
    for c in range(1, chunks - 1):
        landed(c)
    others = pcol_out.at[pl.ds(0, members - 1)]
    pltpu.make_async_copy(others, others, recv_halo).wait()
    pltpu.make_async_copy(others, others, send_halo).wait()
    own_halo.wait()
    for copy in state_rows + state_cols + [first, second]:
        copy.wait()
    everything = inb.at[:, :, :, pl.ds(0, (members - 1) * width)]
    pltpu.make_async_copy(everything, everything, send_in).wait()
    pltpu.make_async_copy(everything, everything, send_out).wait()


def exchange(state, direction, inverses, bands, members):
    levels, local_rows, width = state.shape
    chunks = inverses.shape[0]
    high, low, turns, weights = make_tables()
    f32 = jnp.float32
    anywhere = pl.BlockSpec(memory_space=pl.ANY)
    dma = pltpu.SemaphoreType.DMA
    return pl.pallas_call(
        functools.partial(exchange_kernel, bands, members, chunks),
        out_shape=(
            jax.ShapeDtypeStruct(state.shape, f32),
            jax.ShapeDtypeStruct((2, levels, 8, width), f32),
            jax.ShapeDtypeStruct((2, levels, 8, width), f32),
            jax.ShapeDtypeStruct((2, levels * 8, 128), f32),
            jax.ShapeDtypeStruct((members, 8, 128), f32),
        ),
        in_specs=[anywhere] * 7,
        out_specs=(anywhere,) * 5,
        scratch_shapes=[
            pltpu.VMEM((chunks, levels, 8, members * width), f32),
            pltpu.VMEM((chunks, levels, 8, members * width), f32),
            pltpu.VMEM(inverses.shape, jnp.bfloat16),
            pltpu.VMEM(high.shape, jnp.bfloat16),
            pltpu.VMEM(low.shape, jnp.bfloat16),
            pltpu.VMEM(turns.shape, f32),
            pltpu.VMEM(weights.shape, f32),
            pltpu.VMEM((8, levels * 8 * OUTER, 128), f32),
            pltpu.VMEM((levels * 8 * OUTER, 2 * INNER), jnp.bfloat16),
            pltpu.VMEM((levels * 8 * OUTER, 2 * INNER), jnp.bfloat16),
            pltpu.VMEM((levels * 8 * OUTER, INNER), f32),
            pltpu.VMEM((64, OUTER, HALF), f32),
            pltpu.VMEM((2, levels, local_rows, 128), f32),
            pltpu.VMEM((2, levels * 8, 128), f32),
            pltpu.VMEM((members, 8, 128), f32),
            dma((5,)), dma((2,)), dma((chunks,)), dma((chunks,)), dma,
            dma, dma((chunks,)), dma, dma((chunks,)),
            dma((4,)), dma((4,)), dma((2,)), dma((2,)), dma, dma,
        ],
        compiler_params=pltpu.CompilerParams(
            collective_id=0, has_side_effects=True, vmem_limit_bytes=60 << 20
        ),
        name="exchange",
    )(state, direction, inverses, jnp.asarray(high), jnp.asarray(low), jnp.asarray(turns), jnp.asarray(weights))


def face(a, b, pa, pb):
    s, p, d, dp = (a + b, pa + pb, b - a, pb - pa)
    moved = s + step_size * p
    return dp + (0.25 * quad_coef) * (moved * moved * dp + p * (s + moved) * d)


def stencil_kernel(
    members, chunks,
    state, before_s, after_s, pre, before_p, after_p, kappa, srow, prow, scol, pcol, geometry,
    pre_out, jac_out,
):
    j = pl.program_id(0)
    levels, _, width = state.shape
    rows = 8
    turn = lax.rem(128 - 8 * j, 128)
    geo = pltpu.roll(geometry[...], turn, 1)
    row = lax.broadcasted_iota(jnp.int32, (rows, width), 0)
    lane = lax.broadcasted_iota(jnp.int32, (rows, width), 1)
    for level in range(levels):
        west_s = pltpu.roll(scol[0, level * rows : level * rows + rows, :], turn, 1)
        east_s = pltpu.roll(scol[1, level * rows : level * rows + rows, :], turn, 1)
        tiles_s = [jnp.where(j == 0, srow[0, level], before_s[level])]
        tiles_p = [jnp.where(j == 0, prow[0, level], before_p[level])]
        for c in range(chunks):
            tiles_s.append(state[level, c * rows : c * rows + rows, :])
            tiles_p.append(pre[level, c * rows : c * rows + rows, :])
        last = j == members - 1
        tiles_s.append(jnp.where(last, srow[1, level], after_s[level]))
        tiles_p.append(jnp.where(last, prow[1, level], after_p[level]))

        def ahead(tiles, c):
            return jnp.where(row == rows - 1, pltpu.roll(tiles[c + 1], rows - 1, 0), pltpu.roll(tiles[c], rows - 1, 0))

        def north_face(c):
            return face(tiles_s[c], ahead(tiles_s, c), tiles_p[c], ahead(tiles_p, c))

        below = pltpu.roll(north_face(0), 1, 0)
        for c in range(chunks):
            w, p = (tiles_s[c + 1], tiles_p[c + 1])
            at = c * 4 + level * 2
            line = slice(c * rows, c * rows + rows)
            w_east = jnp.where(lane == width - 1, east_s[:, c : c + 1], pltpu.roll(w, width - 1, 1))
            p_east = jnp.where(lane == width - 1, pcol[0, :, at + 1 : at + 2], pltpu.roll(p, width - 1, 1))
            east = face(w, w_east, p, p_east)
            edge = face(west_s[:, c : c + 1], w[:, :1], pcol[0, :, at : at + 1], p[:, :1])
            west = jnp.where(lane == 0, edge, pltpu.roll(east, 1, 1))
            north = north_face(c + 1)
            turned = pltpu.roll(north, 1, 0)
            south = jnp.where(row == 0, below, turned)
            below = turned
            spread = geo[line, 0:1] * (east - west) + (geo[line, 1:2] * north - geo[line, 2:3] * south)
            pre_out[level, line, :] = p
            jac_out[level, line, :] = p - kappa[line, :].astype(jnp.float32) * spread


def stencil(state, pre, diffusivity, srow, prow, scol, pcol, geometry, members):
    levels, local_rows, width = state.shape
    share = local_rows // members
    chunks = share // 8
    final = local_rows // 8 - 1
    block = pl.BlockSpec((levels, share, width), lambda j: (0, j, 0))
    before = pl.BlockSpec((levels, 8, width), lambda j: (0, jnp.maximum(j * chunks - 1, 0), 0))
    after = pl.BlockSpec((levels, 8, width), lambda j: (0, jnp.minimum(j * chunks + chunks, final), 0))

    def whole(x):
        return pl.BlockSpec(x.shape, lambda j: (0,) * x.ndim)

    return pl.pallas_call(
        functools.partial(stencil_kernel, members, chunks),
        grid=(members,),
        out_shape=(jax.ShapeDtypeStruct(state.shape, jnp.float32),) * 2,
        in_specs=[
            block, before, after, block, before, after,
            pl.BlockSpec((share, width), lambda j: (j, 0)),
            whole(srow), whole(prow), whole(scol),
            pl.BlockSpec((1, 8, 128), lambda j: (j, 0, 0)),
            whole(geometry),
        ],
        out_specs=(block, block),
        compiler_params=pltpu.CompilerParams(vmem_limit_bytes=48 << 20),
        name="stencil",
    )(state, state, state, pre, pre, pre, diffusivity, srow, prow, scol, pcol, geometry)


def on_device(bands, members, state, direction, diffusivity, inverses):
    local_rows = state.shape[1]
    pre, srow, prow, scol, pcol = exchange(state, direction, inverses, bands, members)
    table = jnp.asarray(make_geometry(bands, members, local_rows // members))
    geometry = lax.dynamic_index_in_dim(table, lax.axis_index("lat"), 0, keepdims=False)
    return stencil(state, pre, diffusivity, srow, prow, scol, pcol, geometry, members)


def solution(mesh):
    return jax.shard_map(
        functools.partial(on_device, mesh.shape["lat"], mesh.shape["lon"]),
        mesh=mesh,
        in_specs=(
            P(None, "lat", "lon"),
            P(None, "lat", "lon"),
            P("lat", "lon"),
            P(("lat", "lon"), None, None, None, None),
        ),
        out_specs=(P(None, "lat", "lon"), P(None, "lat", "lon")),
        check_vma=False,
    )
```

time: 312 us -> 152 us (0.49); the launches traced: 307 us -> 151 us
  Pallas kernels: 0 us -> 144 us
  other arithmetic: 72.7 us -> 0 us
  waiting for transfers between devices: 69.6 us -> 0 us
  matrix products: 56.5 us -> 0 us
  local copies, waits for them, and re-layouts: 50.8 us -> 6.42 us
  blocking collectives: 34.9 us -> 0 us
  starting transfers between devices: 21.6 us -> 0 us
    pallas_call x0 -> x2, Pallas kernels: none -> 144 us  [the longest x1 118 us: exchange(): pl.pallas_call(functools.partial(exchange_kernel, bands, members, chunks)...]
    all_to_all x2 -> x0, waiting for transfers between devices: 69.5 us -> none  [the longest x1 37.5 us: spectral(): lax.all_to_all(direction, 'lon', split_axis=1, concat_axis=2, tiled=True)]
    dot_general x6 -> x0, matrix products: 56.5 us -> none  [the longest x4 22.5 us: batch_apply(): lax.dot_general(wide, values, (((2,), (1,)), ((0,), (0,))), precision=hig...]
    all_to_all x1 -> x0, blocking collectives: 34.9 us -> none  [several_exchanges(): lax.all_to_all(piece, axis, split_axis=0, concat_axis=0, tiled=True)]
    div x2 -> x0, other arithmetic: 27.6 us -> none  [the longest x1 27 us: on_device(): jacobian_product = (moved - base) / step_size]
    concatenate x3 -> x0, other arithmetic: 17.3 us -> none  [the longest x1 14.5 us: extended(): jnp.concatenate([jnp.pad(low, around), x, jnp.pad(high, around)], axis=dim)]
    all_to_all x2 -> x0, starting transfers between devices: 11.8 us -> none  [the longest x1 7.38 us: spectral(): lax.all_to_all(direction, 'lon', split_axis=1, concat_axis=2, tiled=True)]
    another operation x2 -> x0, local copies, waits for them, and re-layouts: 11.4 us -> none  [split_up(): return jnp.moveaxis(x.reshape(*before, length, -1, *after), dim, 0)]
  transfers between devices with their start and end apart: 6 -> 0, of which waited for: 2 -> 0; matrix products, arithmetic and copies ran while one was open for 9% -> 0% of each run, Pallas kernels for 0% -> 0%
where the time goes in v1:
time: 152 us; the launch traced here: 151 us
  Pallas kernels  144 us (95%)
  local copies, waits for them, and re-layouts  6.42 us (4%)
    pallas_call x1, Pallas kernels, exchange(): pl.pallas_call(functools.partial(exchange_kernel, bands, members, chunks)...  118 us
    pallas_call x1, Pallas kernels, stencil(): pl.pallas_call(functools.partial(stencil_kernel, members, chunks), grid=(...  26.7 us
    unnamed x12, local copies, waits for them, and re-layouts  5.68 us

profile of v1, /device:TPU:0, one launch (start us, length us, event | category | flops | bytes accessed | tf_op | source)
XLA Modules:
  0.0 151.4 jit_solution(6996270316736691568)
XLA Ops:
  0.6 0.7 dynamic-slice_bitcast_fusion.geometry
  1.4 0.0 copy-start.1
  1.4 117.6 %exchange.1 = (f32[2,768,768]{2,1,0:T(8,128)}, f32[2,2,8,768]{3,2,1,0:T(8,128)}, f32[2,2,8,768]{3,2,1,0:T(8,128)}, f32[2,16,128]{2,1,0:T(8,128)}, f32[16,8,128]{2,1,0:T(8,128)}) custom-call(f32[2,768,768]{2,1,0:T(8,128)} %after_s.1, f32[2,768,768]{2,1,0:T(8,128)} %direction.1, bf16[6,8,8,24,256]{4,3,2,1,0:T(8,128)(2,1)} %inverses.1, ...), custom_call_target="tpu_custom_call" | custom-call | tf_op jit(solution)/shard_map/exchange/pallas_call | solution.py:421
  119.0 0.0 copy-done.1
  119.0 0.0 copy-start
  119.0 2.3 %copy-done = f32[2,768,768]{2,1,0:T(8,128)S(1)} copy-done((f32[2,768,768]{2,1,0:T(8,128)S(1)}, f32[2,768,768]{2,1,0:T(8,128)}, u32[]{:S(2)}) %copy-start) | copy-done | bytes 4718616
  121.4 0.0 copy-start.2
  121.4 0.9 copy-done.2
  122.3 0.0 copy-start.3
  122.3 0.9 copy-done.3
  123.2 0.0 copy-start.4
  123.2 0.8 copy-done.4
  124.0 0.0 copy-start.5
  124.0 0.7 copy-done.5
  124.7 26.7 %stencil.1 = (f32[2,768,768]{2,1,0:T(8,128)}, f32[2,768,768]{2,1,0:T(8,128)}) custom-call(f32[2,768,768]{2,1,0:T(8,128)S(1)} %copy-done, f32[2,768,768]{2,1,0:T(8,128)S(1)} %copy-done, f32[2,768,768]{2,1,0:T(8,128)S(1)} %copy-done, f32[2,768,768]{2,1,0:T(8,128)} %get-tuple-element.7.pre.before_p.after_p, ...), custom_call_target="tpu_custom_call" | custom-call | tf_op jit(solution)/shard_map/stencil/pallas_call | solution.py:526
Async XLA Ops:
  1.4 117.6 %copy-start.1 = (bf16[768,768]{1,0:T(8,128)(2,1)S(1)}, bf16[768,768]{1,0:T(8,128)(2,1)}, u32[]{:S(2)}) copy-start(bf16[768,768]{1,0:T(8,128)(2,1)} %kappa.1) | copy-start | bytes 3538948
  119.0 2.3 %copy-start = (f32[2,768,768]{2,1,0:T(8,128)S(1)}, f32[2,768,768]{2,1,0:T(8,128)}, u32[]{:S(2)}) copy-start(f32[2,768,768]{2,1,0:T(8,128)} %after_s.1) | copy-start | bytes 14155780
  121.4 0.9 copy-start.2
  122.3 0.9 copy-start.3
  123.2 0.8 copy-start.4
  124.0 0.7 copy-start.5

commit v2 on v1

v2 whole, which is shorter than its diff:
```python
import functools
import math
import jax
import jax.numpy as jnp
import ml_dtypes
import numpy as np
from jax import lax
from jax.experimental import pallas as pl
from jax.experimental.pallas import tpu as pltpu
from jax.sharding import PartitionSpec as P

OUTER = 24
INNER = 512
HALF = 256


def real_dft(xs):
    n = len(xs)
    if n == 3:
        a, b, c = xs
        t = b + c
        return [(a + t, None), (a - 0.5 * t, (c - b) * math.sin(math.pi / 3))]
    even, odd = (real_dft(xs[0::2]), real_dft(xs[1::2]))
    half = n // 2
    out = [None] * (half + 1)
    out[0] = (even[0][0] + odd[0][0], None)
    out[half] = (even[0][0] - odd[0][0], None)
    for k in range(1, (half + 1) // 2):
        (er, ei), (pr, pi) = (even[k], odd[k])
        c, s = (math.cos(2 * math.pi * k / n), math.sin(2 * math.pi * k / n))
        tr, ti = (pr * c + pi * s, pi * c - pr * s)
        out[k] = (er + tr, ei + ti)
        out[half - k] = (er - tr, ti - ei)
    if half % 2 == 0:
        out[half // 2] = (even[half // 2][0], -odd[half // 2][0])
    return out


def real_dft_back(zs, n):
    if n == 3:
        (c, _), (e, o) = zs
        t, u = (c - 0.5 * e, o * math.sin(math.pi / 3))
        return [c + e, t - u, t + u]
    half = n // 2
    quarter = half // 2
    even = [(zs[0][0] + zs[half][0], None)]
    odd = [(zs[0][0] - zs[half][0], None)]
    for k in range(1, (half + 1) // 2):
        (er, ei), (pr, pi) = (zs[k], zs[half - k])
        even.append((er + pr, ei - pi))
        dr, di = (er - pr, ei + pi)
        c, s = (math.cos(2 * math.pi * k / n), math.sin(2 * math.pi * k / n))
        odd.append((dr * c - di * s, dr * s + di * c))
    if half % 2 == 0:
        even.append((zs[quarter][0], None))
        odd.append((-zs[quarter][1], None))
    first, second = (real_dft_back(even, half), real_dft_back(odd, half))
    return [v for pair in zip(first, second) for v in pair]


def make_tables():
    length = OUTER * INNER
    b = np.arange(INNER)
    q = np.arange(HALF)
    angle = 2 * np.pi * ((b[:, None] * q[None, :]) % INNER) / INNER
    c, s = (np.cos(angle), np.sin(angle))
    table = np.block([[c, -s], [s, c]])
    high = table.astype(ml_dtypes.bfloat16)
    low = (table - high.astype(np.float64)).astype(ml_dtypes.bfloat16)
    twist = 2 * np.pi * ((np.arange(OUTER)[:, None] * b[None, :]) % length) / length
    scale = 2.0 / length
    turns = np.stack(
        [np.cos(twist), np.sin(twist), scale * np.cos(twist), scale * np.sin(twist)]
    ).astype(np.float32)
    weights = np.ones((OUTER, HALF), np.float32)
    weights[0, 0] = 0.5
    return high, low, turns, weights


def split(x):
    high = x.astype(jnp.bfloat16)
    return high, (x - high.astype(jnp.float32)).astype(jnp.bfloat16)


def spectral_chunk(inb, outb, invb, table_hi, table_lo, turns, weights, wide, high, low, narrow, invf):
    levels = 2
    rows = 8

    def widen(k, _):
        invf[k] = invb[k // rows, k % rows].astype(jnp.float32) * weights[...]
        return 0

    lax.fori_loop(0, rows * rows, widen, 0)

    def stage_in(t, _):
        level, tile = (t // 4, t % 4)
        lane = pl.multiple_of(tile * 128, 128)
        xs = [inb[level, :, pl.ds(a * INNER + lane, 128)] for a in range(OUTER)]
        ys = real_dft(xs)
        for p in range(OUTER):
            m = p if p <= OUTER // 2 else OUTER - p
            re, im = ys[m]
            c = turns[0, pl.ds(p, 1), pl.ds(lane, 128)]
            s = turns[1, pl.ds(p, 1), pl.ds(lane, 128)]
            if im is None:
                tr, ti = (re * c, -(re * s))
            elif p <= OUTER // 2:
                tr, ti = (re * c + im * s, im * c - re * s)
            else:
                tr, ti = (re * c - im * s, -(im * c) - re * s)
            where = pl.ds(level * (rows * OUTER) + p, rows, stride=OUTER)
            wide[tile, where, :] = tr
            wide[tile + 4, where, :] = ti
        return 0

    lax.fori_loop(0, 8, stage_in, 0)

    def split_wide(k, _):
        at = pl.ds(pl.multiple_of(k * 32, 32), 32)
        for j in range(8):
            cols = slice(j * 128, j * 128 + 128)
            high[at, cols], low[at, cols] = split(wide[j, at, :])
        return 0

    lax.fori_loop(0, 12, split_wide, 0)

    def forward(n, _):
        cols = pl.ds(pl.multiple_of(n * 256, 256), 256)
        a = jnp.dot(high[...], table_hi[:, cols], preferred_element_type=jnp.float32)
        a += jnp.dot(low[...], table_hi[:, cols], preferred_element_type=jnp.float32)
        a += jnp.dot(high[...], table_lo[:, cols], preferred_element_type=jnp.float32)
        narrow[:, cols] = a
        return 0

    lax.fori_loop(0, 2, forward, 0)

    def solve(t, _):
        pt, lane = (pl.multiple_of((t // 2) * 8, 8), pl.multiple_of((t % 2) * 128, 128))
        spec = [
            [
                narrow[pl.ds((level * rows + s) * OUTER + pt, 8), pl.ds(part * HALF + lane, 128)]
                for level in range(levels)
                for part in range(2)
            ]
            for s in range(rows)
        ]
        for r in range(rows):
            total = [None] * 4
            for s in range(rows):
                factor = invf[r * rows + s, pl.ds(pt, 8), pl.ds(lane, 128)]
                for i in range(4):
                    term = factor * spec[s][i]
                    total[i] = term if total[i] is None else total[i] + term
            for i in range(4):
                level, part = (i // 2, i % 2)
                wide[part * 2 + t % 2, pl.ds((level * rows + r) * OUTER + pt, 8), :] = total[i]
        return 0

    lax.fori_loop(0, 6, solve, 0)

    def split_solved(k, _):
        at = pl.ds(pl.multiple_of(k * 32, 32), 32)
        for j in range(4):
            cols = slice(j * 128, j * 128 + 128)
            high[at, cols], low[at, cols] = split(wide[j, at, :])
        return 0

    lax.fori_loop(0, 12, split_solved, 0)

    def backward(n, _):
        cols = pl.ds(pl.multiple_of(n * 256, 256), 256)
        dims = (((1,), (1,)), ((), ()))
        hi, lo = (high[:, : 2 * HALF], low[:, : 2 * HALF])
        a = lax.dot_general(hi, table_hi[cols, :], dims, preferred_element_type=jnp.float32)
        a += lax.dot_general(lo, table_hi[cols, :], dims, preferred_element_type=jnp.float32)
        a += lax.dot_general(hi, table_lo[cols, :], dims, preferred_element_type=jnp.float32)
        wide[2 * n] = a[:, :128]
        wide[2 * n + 1] = a[:, 128:]
        return 0

    lax.fori_loop(0, 4, backward, 0)

    def stage_out(t, _):
        level, tile = (t // 4, t % 4)
        lane = pl.multiple_of(tile * 128, 128)

        def turned(p):
            where = pl.ds(level * (rows * OUTER) + p, rows, stride=OUTER)
            re = wide[tile, where, :]
            im = wide[tile + 4, where, :]
            c = turns[2, pl.ds(p, 1), pl.ds(lane, 128)]
            s = turns[3, pl.ds(p, 1), pl.ds(lane, 128)]
            return re * c - im * s, re * s + im * c

        zs = []
        for p in range(OUTER // 2 + 1):
            re, im = turned(p)
            if 0 < p < OUTER // 2:
                other_re, other_im = turned(OUTER - p)
                re, im = (re + other_re, im - other_im)
            zs.append((re, im))
        for a, v in enumerate(real_dft_back(zs, OUTER)):
            outb[level, a * (INNER // 128) + tile] = v
        return 0

    lax.fori_loop(0, 8, stage_out, 0)


zonal_tau = 0.1
merid_tau = 0.5
zonal_cap = 16.0
quad_coef = 0.25
step_size = 0.01
LIMIT = 36
MESH = pl.DeviceIdType.MESH


def make_geometry(bands, members, rows_each):
    total = bands * members * rows_each
    row = np.arange(total, dtype=np.float64)
    cell = np.sin(np.pi * (row + 0.5) / total)
    low = np.where(row > 0, np.sin(np.pi * row / total), 0.0)
    high = np.where(row + 1 < total, np.sin(np.pi * (row + 1) / total), 0.0)
    zonal = zonal_tau * np.minimum(1.0 / (cell * cell), zonal_cap)
    kinds = np.stack([zonal, merid_tau * high / cell, merid_tau * low / cell], -1)
    kinds = (0.25 * quad_coef) * kinds.reshape(bands, members, rows_each, 3)
    table = np.zeros((bands, rows_each + members, members, 8), np.float32)
    table[:, :rows_each, :, :3] = kinds.transpose(0, 2, 1, 3)
    table = table.reshape(bands, rows_each + members, members * 8)
    table[:, rows_each:, 0] = kinds[:, :, rows_each - 17, 1]
    table[:, rows_each:, 1] = kinds[:, :, rows_each - 8, 2]
    return table


def face(a, b, pa, pb):
    s, p, d, dp = (a + b, pa + pb, b - a, pb - pa)
    moved = s + step_size * p
    return (4.0 / quad_coef + moved * moved) * dp + p * (s + moved) * d


def stencil_tile(j, c, chunks, field, pre, kappa, scol, pcol, geometry, jac, skip="", target=None):
    levels, tiles = field.shape[:2]
    rows = 8
    line = pl.multiple_of((j * chunks + c) * rows, rows)
    base = line + rows
    own = pl.ds(pl.multiple_of(c * rows, rows), rows)
    target = line if target is None else pl.multiple_of(target, rows)
    lane = lax.broadcasted_iota(jnp.int32, (rows, 128), 1)
    first, last = (lane == 0, lane == 127)
    row = lax.broadcasted_iota(jnp.int32, (rows, 128), 0)
    geo = pltpu.roll(geometry[own, :], lax.rem(128 - 8 * j, 128), 1)
    zonal, above, below = [jnp.broadcast_to(geo[:, i : i + 1], (rows, 128)) for i in range(3)]

    def to_end(tile, at):
        return pltpu.roll(tile, lax.rem(255 - at, 128), 1)

    for level in range(levels):
        side = slice(level * rows, level * rows + rows)
        w = [field[level, k, pl.ds(base, rows), :] for k in range(tiles)]
        p = [pre[level, k, pl.ds(base, rows), :] for k in range(tiles)]
        rw = [pltpu.roll(x, 127, 1) for x in w] + [to_end(scol[1, side, :], 8 * j + c)]
        rp = [pltpu.roll(x, 127, 1) for x in p] + [to_end(pcol[j], 4 * c + 2 * level + 1)]
        edge = face(
            to_end(scol[0, side, :], 8 * j + c), rw[0], to_end(pcol[j], 4 * c + 2 * level), rp[0]
        )
        behind = pltpu.roll(edge, 1, 1)
        for k in range(tiles):
            east = face(
                w[k], jnp.where(last, rw[k + 1], rw[k]), p[k], jnp.where(last, rp[k + 1], rp[k])
            )
            turned = pltpu.roll(east, 1, 1)
            west = jnp.where(first, behind, turned)
            behind = turned
            if skip == "north":
                p_north = pltpu.roll(p[k], rows - 1, 0)
            else:
                p_north = pre[level, k, pl.ds(base + 1, rows), :]
            if skip == "south":
                p_south = pltpu.roll(p[k], 1, 0)
            else:
                p_south = pre[level, k, pl.ds(base - 1, rows), :]
            north = above * face(w[k], field[level, k, pl.ds(base + 1, rows), :], p[k], p_north)
            south = below * face(field[level, k, pl.ds(base - 1, rows), :], w[k], p_south, p[k])
            if skip == "north":
                north = jnp.where(row == rows - 1, 0.0, north)
            if skip == "south":
                south = jnp.where(row == 0, 0.0, south)
            spread = zonal * (east - west) + (north - south)
            jac[level, k, pl.ds(target, rows), :] = p[k] - kappa[k, pl.ds(line, rows), :] * spread


def exchange_kernel(
    bands, members, chunks,
    state, direction, diffusivity, inverses, table_hi_in, table_lo_in, turns_in, weights_in, geometry_in,
    field, pre, jac, kappa, scol, pcol,
    inb, outb, invb, table_hi, table_lo, turns, weights, geometry, kappa_in,
    wide, high, low, narrow, invf, scol_out, pcol_out, row_out, row_in,
    load_sem, field_sem, own_in, own_out, own_col, send_in, recv_in, send_out, recv_out,
    send_row, recv_row, send_col, recv_col, send_halo, recv_halo,
):
    levels, local_rows, width = state.shape
    rows = 8
    tiles = width // 128
    share = chunks * rows
    la, me = (lax.axis_index("lat"), lax.axis_index("lon"))
    up, down = (lax.rem(la + 1, bands), lax.rem(la + bands - 1, bands))
    east, west = (lax.rem(me + 1, members), lax.rem(me + members - 1, members))

    def peer(k):
        y = lax.rem(me // 4 + k // 4, members // 4)
        x = lax.rem(me // 2 + k // 2, 2)
        core = lax.rem(me + k, 2)
        return y * 4 + x * 2 + core

    def remote(src, dst, send, recv, lat, lon):
        return pltpu.make_async_remote_copy(
            src_ref=src, dst_ref=dst, send_sem=send, recv_sem=recv,
            device_id=(lat, lon), device_id_type=MESH,
        )

    barrier = pltpu.get_barrier_semaphore()
    for k in range(1, members):
        pl.semaphore_signal(barrier, inc=1, device_id=(la, peer(k)), device_id_type=MESH)
    for lat in (up, down):
        pl.semaphore_signal(barrier, inc=1, device_id=(lat, me), device_id_type=MESH)

    field_copies = [
        pltpu.make_async_copy(
            state.at[:, :, pl.ds(k * 128, 128)], field.at[:, k, pl.ds(rows, local_rows), :], field_sem.at[k]
        )
        for k in range(tiles)
    ]
    kappa_copies = [
        pltpu.make_async_copy(diffusivity.at[:, pl.ds(k * 128, 128)], kappa_in.at[k], field_sem.at[tiles + k])
        for k in range(tiles)
    ]
    loads = [
        pltpu.make_async_copy(src, dst, load_sem.at[i])
        for i, (src, dst) in enumerate(
            (
                (table_hi_in, table_hi), (table_lo_in, table_lo), (turns_in, turns),
                (weights_in, weights), (inverses, invb), (geometry_in.at[la], geometry),
            )
        )
    ]
    for copy in field_copies + loads + kappa_copies:
        copy.start()
    pl.semaphore_wait(barrier, members + 1)

    def chunk_of(i):
        return lax.rem(i + chunks - 1, chunks)

    def lines(member, c):
        return pl.ds(pl.multiple_of(member * share + c * rows, rows), rows)

    def landing(member, c):
        return pl.ds(pl.multiple_of(member * share + c * rows + rows, rows), rows)

    def columns(member):
        return pl.ds(pl.multiple_of(member * width, width), width)

    def send_inputs(i, _):
        c = chunk_of(i)
        for k in range(1, members):
            p = peer(k)
            remote(
                direction.at[:, lines(p, c), :], inb.at[c, :, :, columns(me)],
                send_in, recv_in.at[c], la, p,
            ).start()
        pltpu.make_async_copy(
            direction.at[:, lines(me, c), :], inb.at[c, :, :, columns(me)], own_in.at[c]
        ).start()
        return 0

    lax.fori_loop(0, chunks, send_inputs, 0)

    lane = lax.broadcasted_iota(jnp.int32, (rows, 128), 1)
    for copy in field_copies:
        copy.wait()
    scol_out[...] = jnp.zeros_like(scol_out)

    def pack_state(t, _):
        at = (t // chunks) * 8 + lax.rem(t, chunks)
        for side, (k, spot) in enumerate(((0, 0), (tiles - 1, 127))):
            for level in range(levels):
                value = field[level, k, pl.ds(pl.multiple_of(t * rows + rows, rows), rows), :]
                value = pltpu.roll(value, lax.rem(at + 128 - spot, 128), 1)
                line = pl.ds(level * rows, rows)
                scol_out[side, line, :] = jnp.where(lane == at, value, scol_out[side, line, :])
        return 0

    lax.fori_loop(0, members * chunks, pack_state, 0)
    row_out[...] = jnp.zeros_like(row_out)

    def pack_row(source, line, slot):
        for level in range(levels):
            for k in range(tiles):
                at = level * tiles + k
                row_out[slot, at : at + 1, :] = source[level, k, line : line + 1, :]

    def unpack_row(target, line, slot):
        for level in range(levels):
            for k in range(tiles):
                at = level * tiles + k
                target[level, k, line : line + 1, :] = row_in[slot, at : at + 1, :]

    def row_copy(slot, lat):
        return remote(row_out.at[slot], row_in.at[slot], send_row.at[slot], recv_row.at[slot], lat, me)

    top, bottom = (rows + local_rows - 1, rows)
    pack_row(field, top, 0)
    pack_row(field, bottom, 1)
    pcol_out[...] = jnp.zeros_like(pcol_out)
    small = [
        remote(scol_out.at[1], scol.at[0], send_col.at[0], recv_col.at[0], la, east),
        remote(scol_out.at[0], scol.at[1], send_col.at[1], recv_col.at[1], la, west),
        row_copy(0, up),
        row_copy(1, down),
    ]
    for copy in small:
        copy.start()
    for copy in kappa_copies:
        copy.wait()

    def widen_kappa(t, _):
        at = pl.ds(pl.multiple_of(t * 32, 32), 32)
        for k in range(tiles):
            kappa[k, at, :] = kappa_in[k, at, :].astype(jnp.float32)
        return 0

    lax.fori_loop(0, local_rows // 32, widen_kappa, 0)
    for copy in loads:
        copy.wait()

    def chunk(i, _):
        c = chunk_of(i)
        part = inb.at[c, :, :, pl.ds(0, (members - 1) * width)]
        pltpu.make_async_copy(part, part, recv_in.at[c]).wait()
        pltpu.make_async_copy(
            direction.at[:, lines(me, c), :], inb.at[c, :, :, columns(me)], own_in.at[c]
        ).wait()
        spectral_chunk(
            inb.at[c], outb.at[c], invb.at[c], table_hi, table_lo, turns, weights,
            wide, high, low, narrow, invf,
        )

        slot = i // (chunks - 1)

        def pack(d, _):
            before = lax.rem(d * tiles + members * tiles - 1, members * tiles)
            after = lax.rem(d * tiles + tiles, members * tiles)
            held = pcol_out[slot, d]
            for level in range(levels):
                for side, (source, spot) in enumerate(((before, 127), (after, 0))):
                    at = c * 4 + level * 2 + side
                    value = pltpu.roll(outb[c, level, source], lax.rem(at + 128 - spot, 128), 1)
                    held = jnp.where(lane == at, value, held)
            pcol_out[slot, d] = held
            return 0

        lax.fori_loop(0, members, pack, 0)

        @pl.when(i >= chunks - 2)
        def _():
            for k in range(1, members):
                p = peer(k)
                remote(
                    pcol_out.at[slot, p], pcol.at[slot, me], send_halo.at[slot], recv_halo.at[slot], la, p
                ).start()
            pltpu.make_async_copy(pcol_out.at[slot, me], pcol.at[slot, me], own_col.at[slot]).start()

        for k in range(1, members):
            p = peer(k)
            remote(
                outb.at[c, :, pl.ds(p * tiles, tiles)], pre.at[:, :, landing(me, c), :],
                send_out, recv_out.at[c], la, p,
            ).start()
        pltpu.make_async_copy(
            outb.at[c, :, pl.ds(me * tiles, tiles)], pre.at[:, :, landing(me, c), :], own_out.at[c]
        ).start()
        return 0

    lax.fori_loop(0, chunks, chunk, 0)

    def landed(c):
        part = outb.at[c, :, pl.ds(0, (members - 1) * tiles)]
        pltpu.make_async_copy(part, part, recv_out.at[c]).wait()
        pltpu.make_async_copy(
            outb.at[c, :, pl.ds(me * tiles, tiles)], pre.at[:, :, landing(me, c), :], own_out.at[c]
        ).wait()

    def stencil(c, low, high, skip=""):
        def one(j, _):
            stencil_tile(j, c, chunks, field, pre, kappa, scol, pcol.at[0], geometry, jac, skip)
            return 0

        lax.fori_loop(low, high, one, 0)

    def halo(slot):
        others = pcol_out.at[slot, pl.ds(0, members - 1)]
        pltpu.make_async_copy(others, others, recv_halo.at[slot]).wait()
        pltpu.make_async_copy(pcol_out.at[slot, me], pcol.at[slot, me], own_col.at[slot]).wait()
        pltpu.make_async_copy(others, others, send_halo.at[slot]).wait()

    final = chunks - 1
    for copy in small:
        copy.wait()
    unpack_row(field, bottom - 1, 0)
    unpack_row(field, top + 1, 1)
    landed(final)
    pack_row(pre, top, 2)
    first = row_copy(2, up)
    first.start()
    landed(0)
    pack_row(pre, bottom, 3)
    second = row_copy(3, down)
    second.start()
    for c in range(1, chunks - 3):
        landed(c)
    halo(0)
    stencil(0, 1, members)
    lax.fori_loop(1, chunks - 4, lambda c, _: (stencil(c, 0, members), 0)[1], 0)
    stencil(final, 0, members - 1, "south")
    landed(chunks - 3)
    stencil(chunks - 4, 0, members)
    stencil(chunks - 3, 0, members, "north")
    first.wait()
    second.wait()
    unpack_row(pre, bottom - 1, 2)
    unpack_row(pre, top + 1, 3)
    stencil(0, 0, 1)
    stencil(final, members - 1, members, "south")
    landed(chunks - 2)
    halo(1)
    part = inb.at[:, :, :, pl.ds(0, (members - 1) * width)]
    pltpu.make_async_copy(part, part, send_in).wait()
    part = outb.at[:, :, pl.ds(0, (members - 1) * tiles)]
    pltpu.make_async_copy(part, part, send_out).wait()


def finish_kernel(
    members, chunks, field, pre, jac, kappa, scol, pcol, geometry_in,
    pre_out, jac_out, work, geometry, geo_sem, pre_sem, early_sem, late_sem,
):
    levels, tiles = field.shape[:2]
    rows = 8
    share = chunks * rows
    late = 3 * rows
    early = share - late
    geo = pltpu.make_async_copy(geometry_in.at[lax.axis_index("lat")], geometry, geo_sem)
    geo.start()
    count = members * share

    def lane_tile(k):
        return pl.ds(k * 128, 128)

    pre_copies = [
        pltpu.make_async_copy(
            pre.at[:, k, pl.ds(rows, count), :], pre_out.at[:, :, lane_tile(k)], pre_sem.at[k]
        )
        for k in range(tiles)
    ]

    def early_copy(j, k):
        line = pl.ds(pl.multiple_of(j * share, rows), early)
        return pltpu.make_async_copy(
            jac.at[:, k, line, :], jac_out.at[:, line, lane_tile(k)], early_sem.at[k, j]
        )

    def late_copy(j, k):
        line = pl.ds(pl.multiple_of(j * share + early, rows), late)
        return pltpu.make_async_copy(
            work.at[:, k, pl.ds(pl.multiple_of(j * late, rows), late), :],
            jac_out.at[:, line, lane_tile(k)], late_sem.at[k, j],
        )

    def start_early(j, _):
        for k in range(tiles):
            early_copy(j, k).start()
        return 0

    geo.wait()
    for copy in pre_copies:
        copy.start()
    lax.fori_loop(0, members, start_early, 0)

    def group(g, _):
        def take(j, _):
            for level in range(levels):
                for k in range(tiles):
                    for at in (0, late - rows):
                        source = pl.ds(pl.multiple_of(j * share + early + at, rows), rows)
                        target = pl.ds(pl.multiple_of(j * late + at, rows), rows)
                        work[level, k, target, :] = jac[level, k, source, :]
            return 0

        lax.fori_loop(g * rows, g * rows + rows, take, 0)
        factor = geometry[pl.ds(pl.multiple_of(share + g * rows, rows), rows), :]
        above, below = [jnp.broadcast_to(factor[:, i : i + 1], (rows, 128)) for i in range(2)]

        def every(at, padded=0):
            return pl.ds(g * rows * share + early + at + padded, rows, stride=share)

        for level in range(levels):
            for k in range(tiles):
                def pair(at):
                    lower, upper = (every(at, rows), every(at + 1, rows))
                    return face(field[level, k, lower, :], field[level, k, upper, :], pre[level, k, lower, :], pre[level, k, upper, :])

                low_at, high_at = (rows - 1, late - rows)
                fixed = jac[level, k, every(low_at), :] - kappa[k, every(low_at), :] * (above * pair(low_at))
                work[level, k, pl.ds(g * rows * late + low_at, rows, stride=late), :] = fixed
                fixed = jac[level, k, every(high_at), :] + kappa[k, every(high_at), :] * (below * pair(high_at - 1))
                work[level, k, pl.ds(g * rows * late + high_at, rows, stride=late), :] = fixed

        def one(j, _):
            stencil_tile(
                j, chunks - 2, chunks, field, pre, kappa, scol, pcol.at[1], geometry,
                work, "", j * late + rows,
            )
            for k in range(tiles):
                late_copy(j, k).start()
            return 0

        lax.fori_loop(g * rows, g * rows + rows, one, 0)
        return 0

    lax.fori_loop(0, members // rows, group, 0)

    def drain(j, _):
        for k in range(tiles):
            early_copy(j, k).wait()
            late_copy(j, k).wait()
        return 0

    lax.fori_loop(0, members, drain, 0)
    for copy in pre_copies:
        copy.wait()


def on_device(bands, members, state, direction, diffusivity, inverses):
    levels, local_rows, width = state.shape
    chunks = inverses.shape[0]
    tiles = width // 128
    share = local_rows // members
    table_hi, table_lo, turns, weights = make_tables()
    geometry = jnp.asarray(make_geometry(bands, members, share))
    f32 = jnp.float32
    anywhere = pl.BlockSpec(memory_space=pl.ANY)
    on_chip = pl.BlockSpec(memory_space=pltpu.VMEM)
    dma = pltpu.SemaphoreType.DMA
    padded = (levels, tiles, local_rows + 16, 128)
    parts = pl.pallas_call(
        functools.partial(exchange_kernel, bands, members, chunks),
        out_shape=(
            pltpu.VMEM(padded, f32),
            pltpu.VMEM(padded, f32),
            pltpu.VMEM((levels, tiles, local_rows, 128), f32),
            pltpu.VMEM((tiles, local_rows, 128), f32),
            pltpu.VMEM((2, levels * 8, 128), f32),
            pltpu.VMEM((2, members, 8, 128), f32),
        ),
        in_specs=[pl.BlockSpec(memory_space=pltpu.HBM)] * 9,
        out_specs=(on_chip,) * 6,
        scratch_shapes=[
            pltpu.VMEM((chunks, levels, 8, members * width), f32),
            pltpu.VMEM((chunks, levels, members * tiles, 8, 128), f32),
            pltpu.VMEM(inverses.shape, jnp.bfloat16),
            pltpu.VMEM(table_hi.shape, jnp.bfloat16),
            pltpu.VMEM(table_lo.shape, jnp.bfloat16),
            pltpu.VMEM(turns.shape, f32),
            pltpu.VMEM(weights.shape, f32),
            pltpu.VMEM(geometry.shape[1:], f32),
            pltpu.VMEM((tiles, local_rows, 128), jnp.bfloat16),
            pltpu.VMEM((8, levels * 8 * OUTER, 128), f32),
            pltpu.VMEM((levels * 8 * OUTER, 2 * INNER), jnp.bfloat16),
            pltpu.VMEM((levels * 8 * OUTER, 2 * INNER), jnp.bfloat16),
            pltpu.VMEM((levels * 8 * OUTER, INNER), f32),
            pltpu.VMEM((64, OUTER, HALF), f32),
            pltpu.VMEM((2, levels * 8, 128), f32),
            pltpu.VMEM((2, members, 8, 128), f32),
            pltpu.VMEM((4, 16, 128), f32),
            pltpu.VMEM((4, 16, 128), f32),
            dma((6,)), dma((2 * tiles,)), dma((chunks,)), dma((chunks,)), dma((2,)),
            dma, dma((chunks,)), dma, dma((chunks,)),
            dma((4,)), dma((4,)), dma((2,)), dma((2,)), dma((2,)), dma((2,)),
        ],
        compiler_params=pltpu.CompilerParams(
            collective_id=0, has_side_effects=True, vmem_limit_bytes=LIMIT << 20
        ),
        name="exchange",
    )(
        *[
            pltpu.with_memory_space_constraint(jnp.asarray(x), pltpu.HBM)
            for x in (state, direction, diffusivity, inverses, table_hi, table_lo, turns, weights, geometry)
        ]
    )
    return pl.pallas_call(
        functools.partial(finish_kernel, members, chunks),
        out_shape=(jax.ShapeDtypeStruct(state.shape, f32),) * 2,
        in_specs=[on_chip] * 6 + [pl.BlockSpec(memory_space=pltpu.HBM)],
        out_specs=(anywhere,) * 2,
        scratch_shapes=[
            pltpu.VMEM((levels, tiles, members * 24, 128), f32),
            pltpu.VMEM(geometry.shape[1:], f32),
            dma, dma((tiles,)), dma((tiles, members)), dma((tiles, members)),
        ],
        compiler_params=pltpu.CompilerParams(vmem_limit_bytes=8 << 20),
        name="finish",
    )(*parts, geometry)


def solution(mesh):
    return jax.shard_map(
        functools.partial(on_device, mesh.shape["lat"], mesh.shape["lon"]),
        mesh=mesh,
        in_specs=(
            P(None, "lat", "lon"),
            P(None, "lat", "lon"),
            P("lat", "lon"),
            P(("lat", "lon"), None, None, None, None),
        ),
        out_specs=(P(None, "lat", "lon"), P(None, "lat", "lon")),
        check_vma=False,
    )
```

time: 152 us -> 124 us (0.82)
  Pallas kernels: 144 us -> 123 us
  local copies, waits for them, and re-layouts: 6.42 us -> 0.01 us
    pallas_call x2, Pallas kernels: 144 us -> 123 us  [the longest x1 116 us: on_device(): pl.pallas_call(functools.partial(exchange_kernel, bands, members, chunks)...]
    unnamed x12 -> x2, local copies, waits for them, and re-layouts: 5.68 us -> 0.01 us
where the time goes in v2:
time: 124 us; the launch traced here: 123 us
  Pallas kernels  123 us (99%)
    pallas_call x1, Pallas kernels, on_device(): pl.pallas_call(functools.partial(exchange_kernel, bands, members, chunks)...  116 us
    pallas_call x1, Pallas kernels, on_device(): pl.pallas_call(functools.partial(finish_kernel, members, chunks), out_sha...  6.96 us

profile of v2, /device:TPU:0, one launch (start us, length us, event | category | flops | bytes accessed | tf_op | source)
XLA Modules:
  0.0 123.4 jit_solution(16178648683872513414)
XLA Ops:
  0.6 0.0 copy-start
  0.6 115.7 %exchange.1 = (f32[2,6,784,128]{3,2,1,0:T(8,128)S(1)}, f32[2,6,784,128]{3,2,1,0:T(8,128)S(1)}, f32[2,6,768,128]{3,2,1,0:T(8,128)S(1)}, f32[6,768,128]{2,1,0:T(8,...) custom-call(f32[2,768,768]{2,1,0:T(8,128)} %state.1, f32[2,768,768]{2,1,0:T(8,128)} %direction.1, ...), custom_call_target="tpu_custom_call" | custom-call | tf_op jit(solution)/shard_map/exchange/pallas_call | solution.py:653
  116.4 0.0 copy-done
  116.4 7.0 %finish.1 = (f32[2,768,768]{2,1,0:T(8,128)}, f32[2,768,768]{2,1,0:T(8,128)}) custom-call(f32[2,6,784,128]{3,2,1,0:T(8,128)S(1)} %get-tuple-element.8.field, f32[2,6,784,128]{3,2,1,0:T(8,128)S(1)} %get-tuple-element.9.pre, f32[2,6,768,128]{3,2,1,0:T(8,128)S(1)} %get-tuple-element.10.jac, f32[6,768,128]{2,1,0:T(8,128)S(1)} %get-tuple-element.11.kappa, ...), custom_call_target="tpu_custom_call" | custom-call | tf_op jit(solution)/shard_map/finish/pallas_call | solution.py:698
Async XLA Ops:
  0.6 115.8 %copy-start = (f32[8,64,128]{2,1,0:T(8,128)S(1)}, f32[8,64,128]{2,1,0:T(8,128)}, u32[]{:S(2)}) copy-start(f32[8,64,128]{2,1,0:T(8,128)} %constant.10.clone.geometry_in) | copy-start | bytes 786436

commit v3 on v2

--- a/solution.py
+++ b/solution.py
@@ -212,6 +212,7 @@
 quad_coef = 0.25
 step_size = 0.01
 LIMIT = 36
+GROUP = 4
 MESH = pl.DeviceIdType.MESH
 
 
@@ -238,6 +239,21 @@
     return (4.0 / quad_coef + moved * moved) * dp + p * (s + moved) * d
 
 
+def align_halo(packed, aligned):
+    rows = 8
+    row = lax.broadcasted_iota(jnp.int32, (rows, 128), 0)
+
+    def one(j, _):
+        for level in range(packed.shape[1]):
+            x = jnp.broadcast_to(packed[j, level : level + 1, :], (rows, 128))
+            for bit in (1, 2, 4):
+                x = jnp.where((row // bit) % 2 == 1, pltpu.roll(x, 128 - bit, 1), x)
+            aligned[j, level] = x
+        return 0
+
+    lax.fori_loop(0, packed.shape[0], one, 0, unroll=True)
+
+
 def stencil_tile(j, c, chunks, field, pre, kappa, scol, pcol, geometry, jac, skip="", target=None):
     levels, tiles = field.shape[:2]
     rows = 8
@@ -259,9 +275,9 @@
         w = [field[level, k, pl.ds(base, rows), :] for k in range(tiles)]
         p = [pre[level, k, pl.ds(base, rows), :] for k in range(tiles)]
         rw = [pltpu.roll(x, 127, 1) for x in w] + [to_end(scol[1, side, :], 8 * j + c)]
-        rp = [pltpu.roll(x, 127, 1) for x in p] + [to_end(pcol[j], 4 * c + 2 * level + 1)]
+        rp = [pltpu.roll(x, 127, 1) for x in p] + [to_end(pcol[j, level], (c * 2 + 1) * rows)]
         edge = face(
-            to_end(scol[0, side, :], 8 * j + c), rw[0], to_end(pcol[j], 4 * c + 2 * level), rp[0]
+            to_end(scol[0, side, :], 8 * j + c), rw[0], to_end(pcol[j, level], c * 2 * rows), rp[0]
         )
         behind = pltpu.roll(edge, 1, 1)
         for k in range(tiles):
@@ -292,9 +308,9 @@
 def exchange_kernel(
     bands, members, chunks,
     state, direction, diffusivity, inverses, table_hi_in, table_lo_in, turns_in, weights_in, geometry_in,
-    field, pre, jac, kappa, scol, pcol,
-    inb, outb, invb, table_hi, table_lo, turns, weights, geometry, kappa_in,
-    wide, high, low, narrow, invf, scol_out, pcol_out, row_out, row_in,
+    field, pre, jac, kappa, scol, pcol, geometry,
+    inb, outb, invb, table_hi, table_lo, turns, weights, kappa_in,
+    wide, high, low, narrow, invf, scol_out, pcol_out, row_out, row_in, aligned,
     load_sem, field_sem, own_in, own_out, own_col, send_in, recv_in, send_out, recv_out,
     send_row, recv_row, send_col, recv_col, send_halo, recv_halo,
 ):
@@ -375,6 +391,7 @@
     lax.fori_loop(0, chunks, send_inputs, 0)
 
     lane = lax.broadcasted_iota(jnp.int32, (rows, 128), 1)
+    row = lax.broadcasted_iota(jnp.int32, (rows, 128), 0)
     for copy in field_copies:
         copy.wait()
     scol_out[...] = jnp.zeros_like(scol_out)
@@ -449,13 +466,12 @@
         def pack(d, _):
             before = lax.rem(d * tiles + members * tiles - 1, members * tiles)
             after = lax.rem(d * tiles + tiles, members * tiles)
-            held = pcol_out[slot, d]
             for level in range(levels):
+                held = jnp.zeros((rows, 128), jnp.float32)
                 for side, (source, spot) in enumerate(((before, 127), (after, 0))):
-                    at = c * 4 + level * 2 + side
-                    value = pltpu.roll(outb[c, level, source], lax.rem(at + 128 - spot, 128), 1)
-                    held = jnp.where(lane == at, value, held)
-            pcol_out[slot, d] = held
+                    value = jnp.broadcast_to(outb[c, level, source][:, spot : spot + 1], (rows, 128))
+                    held = jnp.where(lane == (c * 2 + side) * rows + row, value, held)
+                pcol_out[slot, d, level : level + 1, :] += jnp.sum(held, 0, keepdims=True)
             return 0
 
         lax.fori_loop(0, members, pack, 0)
@@ -491,7 +507,7 @@
 
     def stencil(c, low, high, skip=""):
         def one(j, _):
-            stencil_tile(j, c, chunks, field, pre, kappa, scol, pcol.at[0], geometry, jac, skip)
+            stencil_tile(j, c, chunks, field, pre, kappa, scol, aligned, geometry, jac, skip)
             return 0
 
         lax.fori_loop(low, high, one, 0)
@@ -518,6 +534,7 @@
     for c in range(1, chunks - 3):
         landed(c)
     halo(0)
+    align_halo(pcol.at[0], aligned)
     stencil(0, 1, members)
     lax.fori_loop(1, chunks - 4, lambda c, _: (stencil(c, 0, members), 0)[1], 0)
     stencil(final, 0, members - 1, "south")
@@ -539,16 +556,14 @@
 
 
 def finish_kernel(
-    members, chunks, field, pre, jac, kappa, scol, pcol, geometry_in,
-    pre_out, jac_out, work, geometry, geo_sem, pre_sem, early_sem, late_sem,
+    members, chunks, field, pre, jac, kappa, scol, pcol, geometry,
+    pre_out, jac_out, work, aligned, pre_sem, early_sem, late_sem,
 ):
     levels, tiles = field.shape[:2]
     rows = 8
     share = chunks * rows
     late = 3 * rows
     early = share - late
-    geo = pltpu.make_async_copy(geometry_in.at[lax.axis_index("lat")], geometry, geo_sem)
-    geo.start()
     count = members * share
 
     def lane_tile(k):
@@ -561,28 +576,27 @@
         for k in range(tiles)
     ]
 
-    def early_copy(j, k):
-        line = pl.ds(pl.multiple_of(j * share, rows), early)
+    shape = (levels, tiles, members)
+    jac_parts = jac.reshape(*shape, share, 128)
+    work_parts = work.reshape(*shape, late, 128)
+    out_parts = jac_out.reshape(levels, members, share, tiles * 128)
+    early_copies = [
+        pltpu.make_async_copy(
+            jac_parts.at[:, k, :, :early, :], out_parts.at[:, :, :early, lane_tile(k)], early_sem.at[k]
+        )
+        for k in range(tiles)
+    ]
+
+    def late_copy(q, k):
+        some = pl.ds(q * GROUP, GROUP)
         return pltpu.make_async_copy(
-            jac.at[:, k, line, :], jac_out.at[:, line, lane_tile(k)], early_sem.at[k, j]
+            work_parts.at[:, k, some], out_parts.at[:, some, early:, lane_tile(k)], late_sem.at[q, k]
         )
 
-    def late_copy(j, k):
-        line = pl.ds(pl.multiple_of(j * share + early, rows), late)
-        return pltpu.make_async_copy(
-            work.at[:, k, pl.ds(pl.multiple_of(j * late, rows), late), :],
-            jac_out.at[:, line, lane_tile(k)], late_sem.at[k, j],
-        )
-
-    def start_early(j, _):
-        for k in range(tiles):
-            early_copy(j, k).start()
-        return 0
-
-    geo.wait()
-    for copy in pre_copies:
+    for copy in pre_copies + early_copies:
         copy.start()
-    lax.fori_loop(0, members, start_early, 0)
+
+    align_halo(pcol.at[1], aligned)
 
     def group(g, _):
         def take(j, _):
@@ -615,26 +629,29 @@
 
         def one(j, _):
             stencil_tile(
-                j, chunks - 2, chunks, field, pre, kappa, scol, pcol.at[1], geometry,
+                j, chunks - 2, chunks, field, pre, kappa, scol, aligned, geometry,
                 work, "", j * late + rows,
             )
+            return 0
+
+        def some(q, _):
+            lax.fori_loop(q * GROUP, q * GROUP + GROUP, one, 0)
             for k in range(tiles):
-                late_copy(j, k).start()
+                late_copy(q, k).start()
             return 0
 
-        lax.fori_loop(g * rows, g * rows + rows, one, 0)
+        lax.fori_loop(g * (rows // GROUP), (g + 1) * (rows // GROUP), some, 0)
         return 0
 
     lax.fori_loop(0, members // rows, group, 0)
 
-    def drain(j, _):
+    def drain(q, _):
         for k in range(tiles):
-            early_copy(j, k).wait()
-            late_copy(j, k).wait()
-        return 0
-
-    lax.fori_loop(0, members, drain, 0)
-    for copy in pre_copies:
+            late_copy(q, k).wait()
+        return 0
+
+    lax.fori_loop(0, members // GROUP, drain, 0)
+    for copy in pre_copies + early_copies:
         copy.wait()
 
 
@@ -658,10 +675,11 @@
             pltpu.VMEM((levels, tiles, local_rows, 128), f32),
             pltpu.VMEM((tiles, local_rows, 128), f32),
             pltpu.VMEM((2, levels * 8, 128), f32),
-            pltpu.VMEM((2, members, 8, 128), f32),
+            pltpu.VMEM((2, members, levels, 128), f32),
+            pltpu.VMEM(geometry.shape[1:], f32),
         ),
         in_specs=[pl.BlockSpec(memory_space=pltpu.HBM)] * 9,
-        out_specs=(on_chip,) * 6,
+        out_specs=(on_chip,) * 7,
         scratch_shapes=[
             pltpu.VMEM((chunks, levels, 8, members * width), f32),
             pltpu.VMEM((chunks, levels, members * tiles, 8, 128), f32),
@@ -670,7 +688,6 @@
             pltpu.VMEM(table_lo.shape, jnp.bfloat16),
             pltpu.VMEM(turns.shape, f32),
             pltpu.VMEM(weights.shape, f32),
-            pltpu.VMEM(geometry.shape[1:], f32),
             pltpu.VMEM((tiles, local_rows, 128), jnp.bfloat16),
             pltpu.VMEM((8, levels * 8 * OUTER, 128), f32),
             pltpu.VMEM((levels * 8 * OUTER, 2 * INNER), jnp.bfloat16),
@@ -678,9 +695,10 @@
             pltpu.VMEM((levels * 8 * OUTER, INNER), f32),
             pltpu.VMEM((64, OUTER, HALF), f32),
             pltpu.VMEM((2, levels * 8, 128), f32),
-            pltpu.VMEM((2, members, 8, 128), f32),
+            pltpu.VMEM((2, members, levels, 128), f32),
             pltpu.VMEM((4, 16, 128), f32),
             pltpu.VMEM((4, 16, 128), f32),
+            pltpu.VMEM((members, levels, 8, 128), f32),
             dma((6,)), dma((2 * tiles,)), dma((chunks,)), dma((chunks,)), dma((2,)),
             dma, dma((chunks,)), dma, dma((chunks,)),
             dma((4,)), dma((4,)), dma((2,)), dma((2,)), dma((2,)), dma((2,)),
@@ -698,16 +716,16 @@
     return pl.pallas_call(
         functools.partial(finish_kernel, members, chunks),
         out_shape=(jax.ShapeDtypeStruct(state.shape, f32),) * 2,
-        in_specs=[on_chip] * 6 + [pl.BlockSpec(memory_space=pltpu.HBM)],
+        in_specs=[on_chip] * 7,
         out_specs=(anywhere,) * 2,
         scratch_shapes=[
             pltpu.VMEM((levels, tiles, members * 24, 128), f32),
-            pltpu.VMEM(geometry.shape[1:], f32),
-            dma, dma((tiles,)), dma((tiles, members)), dma((tiles, members)),
+            pltpu.VMEM((members, levels, 8, 128), f32),
+            dma((tiles,)), dma((tiles,)), dma((members // GROUP, tiles)),
         ],
         compiler_params=pltpu.CompilerParams(vmem_limit_bytes=8 << 20),
         name="finish",
-    )(*parts, geometry)
+    )(*parts)
 
 
 def solution(mesh):

time: 124 us -> 121 us (0.976)
  Pallas kernels: 123 us -> 120 us
    pallas_call x1, Pallas kernels: 6.96 us -> 5.28 us  [on_device(): pl.pallas_call(functools.partial(finish_kernel, members, chunks), out_sha...]
where the time goes in v3:
time: 121 us
  Pallas kernels  120 us (99%)
    pallas_call x1, Pallas kernels, on_device(): pl.pallas_call(functools.partial(exchange_kernel, bands, members, chunks)...  115 us
    pallas_call x1, Pallas kernels, on_device(): pl.pallas_call(functools.partial(finish_kernel, members, chunks), out_sha...  5.28 us

profile of v3, /device:TPU:0, one launch (start us, length us, event | category | flops | bytes accessed | tf_op | source)
XLA Modules:
  0.0 120.6 jit_solution(10170946524495956058)
XLA Ops:
  0.6 114.7 %exchange.1 = (f32[2,6,784,128]{3,2,1,0:T(8,128)S(1)}, f32[2,6,784,128]{3,2,1,0:T(8,128)S(1)}, f32[2,6,768,128]{3,2,1,0:T(8,128)S(1)}, f32[6,768,128]{2,1,0:T(8,...) custom-call(f32[2,768,768]{2,1,0:T(8,128)} %state.1, ...), custom_call_target="tpu_custom_call" | custom-call | tf_op jit(solution)/shard_map/exchange/pallas_call | solution.py:670
  115.3 5.3 %finish.1 = (f32[2,768,768]{2,1,0:T(8,128)}, f32[2,768,768]{2,1,0:T(8,128)}) custom-call(f32[2,6,784,128]{3,2,1,0:T(8,128)S(1)} %get-tuple-element.9.field, f32[2,6,784,128]{3,2,1,0:T(8,128)S(1)} %get-tuple-element.10.pre, f32[2,6,768,128]{3,2,1,0:T(8,128)S(1)} %get-tuple-element.11.jac, f32[6,768,128]{2,1,0:T(8,128)S(1)} %get-tuple-element.12.kappa, ...), custom_call_target="tpu_custom_call" | custom-call | tf_op jit(solution)/shard_map/finish/pallas_call | solution.py:716

commit v4 on v3

--- a/solution.py
+++ b/solution.py
@@ -308,9 +308,9 @@
 def exchange_kernel(
     bands, members, chunks,
     state, direction, diffusivity, inverses, table_hi_in, table_lo_in, turns_in, weights_in, geometry_in,
-    field, pre, jac, kappa, scol, pcol, geometry,
+    field, pre, jac, kappa, scol, aligned, geometry,
     inb, outb, invb, table_hi, table_lo, turns, weights, kappa_in,
-    wide, high, low, narrow, invf, scol_out, pcol_out, row_out, row_in, aligned,
+    wide, high, low, narrow, invf, scol_out, pcol_out, row_out, row_in, pcol,
     load_sem, field_sem, own_in, own_out, own_col, send_in, recv_in, send_out, recv_out,
     send_row, recv_row, send_col, recv_col, send_halo, recv_halo,
 ):
@@ -547,8 +547,9 @@
     unpack_row(pre, top + 1, 3)
     stencil(0, 0, 1)
     stencil(final, members - 1, members, "south")
+    halo(1)
+    align_halo(pcol.at[1], aligned)
     landed(chunks - 2)
-    halo(1)
     part = inb.at[:, :, :, pl.ds(0, (members - 1) * width)]
     pltpu.make_async_copy(part, part, send_in).wait()
     part = outb.at[:, :, pl.ds(0, (members - 1) * tiles)]
@@ -556,8 +557,8 @@
 
 
 def finish_kernel(
-    members, chunks, field, pre, jac, kappa, scol, pcol, geometry,
-    pre_out, jac_out, work, aligned, pre_sem, early_sem, late_sem,
+    members, chunks, field, pre, jac, kappa, scol, aligned, geometry,
+    pre_out, jac_out, work, pre_sem, early_sem, late_sem,
 ):
     levels, tiles = field.shape[:2]
     rows = 8
@@ -595,8 +596,6 @@
 
     for copy in pre_copies + early_copies:
         copy.start()
-
-    align_halo(pcol.at[1], aligned)
 
     def group(g, _):
         def take(j, _):
@@ -675,7 +674,7 @@
             pltpu.VMEM((levels, tiles, local_rows, 128), f32),
             pltpu.VMEM((tiles, local_rows, 128), f32),
             pltpu.VMEM((2, levels * 8, 128), f32),
-            pltpu.VMEM((2, members, levels, 128), f32),
+            pltpu.VMEM((members, levels, 8, 128), f32),
             pltpu.VMEM(geometry.shape[1:], f32),
         ),
         in_specs=[pl.BlockSpec(memory_space=pltpu.HBM)] * 9,
@@ -698,7 +697,7 @@
             pltpu.VMEM((2, members, levels, 128), f32),
             pltpu.VMEM((4, 16, 128), f32),
             pltpu.VMEM((4, 16, 128), f32),
-            pltpu.VMEM((members, levels, 8, 128), f32),
+            pltpu.VMEM((2, members, levels, 128), f32),
             dma((6,)), dma((2 * tiles,)), dma((chunks,)), dma((chunks,)), dma((2,)),
             dma, dma((chunks,)), dma, dma((chunks,)),
             dma((4,)), dma((4,)), dma((2,)), dma((2,)), dma((2,)), dma((2,)),
@@ -720,7 +719,6 @@
         out_specs=(anywhere,) * 2,
         scratch_shapes=[
             pltpu.VMEM((levels, tiles, members * 24, 128), f32),
-            pltpu.VMEM((members, levels, 8, 128), f32),
             dma((tiles,)), dma((tiles,)), dma((members // GROUP, tiles)),
         ],
         compiler_params=pltpu.CompilerParams(vmem_limit_bytes=8 << 20),

time: 121 us -> 121 us (level)
  no operation moved by 1% of the time
where the time goes in v4:
time: 121 us
  Pallas kernels  120 us (99%)
    pallas_call x1, Pallas kernels, on_device(): pl.pallas_call(functools.partial(exchange_kernel, bands, members, chunks)...  115 us
    pallas_call x1, Pallas kernels, on_device(): pl.pallas_call(functools.partial(finish_kernel, members, chunks), out_sha...  5.03 us

profile of v4, /device:TPU:0, one launch (start us, length us, event | category | flops | bytes accessed | tf_op | source)
XLA Modules:
  0.0 120.6 jit_solution(13492427944501319188)
XLA Ops:
  0.6 114.9 %exchange.1 = (f32[2,6,784,128]{3,2,1,0:T(8,128)S(1)}, f32[2,6,784,128]{3,2,1,0:T(8,128)S(1)}, f32[2,6,768,128]{3,2,1,0:T(8,128)S(1)}, f32[6,768,128]{2,1,0:T(8,...) custom-call(f32[2,768,768]{2,1,0:T(8,128)} %state.1, ...), custom_call_target="tpu_custom_call" | custom-call | tf_op jit(solution)/shard_map/exchange/pallas_call | solution.py:669
  115.6 5.0 %finish.1 = (f32[2,768,768]{2,1,0:T(8,128)}, f32[2,768,768]{2,1,0:T(8,128)}) custom-call(f32[2,6,784,128]{3,2,1,0:T(8,128)S(1)} %get-tuple-element.9.field, f32[2,6,784,128]{3,2,1,0:T(8,128)S(1)} %get-tuple-element.10.pre, f32[2,6,768,128]{3,2,1,0:T(8,128)S(1)} %get-tuple-element.11.jac, f32[6,768,128]{2,1,0:T(8,128)S(1)} %get-tuple-element.12.kappa, ...), custom_call_target="tpu_custom_call" | custom-call | tf_op jit(solution)/shard_map/finish/pallas_call | solution.py:715
